TPU v7x, 32 devices: a whole 2x2x4 slice. The times are simulated.
32 devices in a mesh: row: 2 (over y), col: 8 (over z, core), orient: 2 (over x).
Axes of the slice: x: 2, y: 2, z: 4, core: 2. Of those that a mesh axis runs over, the one named last changes fastest.
Arguments:
- noise: float32 [2, 4096, 4096], P(None, ('row', 'col')), may hold values from -6 to 6
- elevation_library: float32 [16, 128, 128], replicated, may hold values from 0.25 to 1
- tile_choice_index: int32 [32, 32], P('row', 'col'), may hold values from 0 to 15
- family_heading_index: int32 [8], P('orient'), may hold values from 0 to 35
- family_extent_index: int32 [8], P('orient'), may hold values from 0 to 3
Outputs:
- safety_min: float32 [4096, 4096], P('row', ('col', 'orient'))
All inputs are finite; a program needn't handle non-finite values.
Results may differ from a plain program's by a relative error of at most 0.0005.
Values may be sent and summed in bfloat16 or wider, within the bound.
A program may use at most 256 MiB of HBM per device.

v0:
```python
import math

import jax
import jax.numpy as jnp
from jax import lax
from jax.sharding import PartitionSpec as P

R = 8
N_AZ = 36
NSIZE = 4


nugget_share = 0.3
peak_share = 1024.0 / (2.0 * math.pi)
cutoff_ratio = 32.0


def extended(cells, sides, width):
    for axis, dim in sides:
        count = lax.axis_size(axis)
        ends = count - 1
        head = lax.slice_in_dim(cells, 0, width, axis=dim)
        tail = lax.slice_in_dim(cells, cells.shape[dim] - width, cells.shape[dim], axis=dim)
        cells = jnp.concatenate(
            [
                lax.ppermute(tail, axis, [(i, (i + 1) % count) for i in range(ends)]),
                cells,
                lax.ppermute(head, axis, [((i + 1) % count, i) for i in range(ends)]),
            ],
            axis=dim,
        )
    return cells


def partner(x, axis, bit):
    return lax.ppermute(x, axis, [(i, i ^ 1 << bit) for i in range(lax.axis_size(axis))])


def amplitude(u_index, v_index, side_cells):
    wrap_u = jnp.minimum(u_index, side_cells - u_index).astype(jnp.float32)
    wrap_v = jnp.minimum(v_index, side_cells - v_index).astype(jnp.float32)
    cutoff = side_cells / cutoff_ratio
    scaled_u = wrap_u / cutoff
    scaled_v = wrap_v / cutoff
    grown = 1.0 + scaled_u * scaled_u + scaled_v * scaled_v
    spectrum = nugget_share + peak_share / (grown * jnp.sqrt(grown))
    return jnp.sqrt(spectrum) / side_cells


def ellipsoid(offset_u, offset_v, azimuth, size_index):
    heading = azimuth.astype(jnp.float32) * (math.pi / N_AZ)
    semi_axis = R * (size_index.astype(jnp.float32) + (1 + NSIZE)) / (2 * NSIZE)
    across = 0.6 * semi_axis
    slip_depth = 0.3 * semi_axis
    along = offset_u * jnp.cos(heading) + offset_v * jnp.sin(heading)
    lateral = offset_v * jnp.cos(heading) - offset_u * jnp.sin(heading)
    along_part = along / semi_axis
    lateral_part = lateral / across
    inside = 1.0 - along_part * along_part - lateral_part * lateral_part
    height = slip_depth * jnp.sqrt(jnp.maximum(inside, 0.0))
    base_share = jnp.clip(4.0 * inside, 0.0, 1.0)
    return (height, base_share)


def angle_table(row_count, col_count, period):
    left_index = lax.broadcasted_iota(jnp.int32, (row_count, col_count), 0)
    right_index = lax.broadcasted_iota(jnp.int32, (row_count, col_count), 1)
    phase_step = left_index * right_index % period
    angles = phase_step.astype(jnp.float32) * (2.0 * math.pi / period)
    return (jnp.cos(angles), jnp.sin(angles))


def transform_last(real_part, imag_part):
    length = real_part.shape[-1]
    inner_size = 128
    outer_size = length // inner_size
    leading = real_part.shape[:-1]
    real_in = real_part.reshape(leading + (outer_size, inner_size))
    imag_in = imag_part.reshape(leading + (outer_size, inner_size))
    highest = lax.Precision.HIGHEST
    outer_cos, outer_sin = angle_table(outer_size, outer_size, outer_size)
    real_mid = jnp.einsum("...pq,pk->...kq", real_in, outer_cos, precision=highest) + jnp.einsum(
        "...pq,pk->...kq", imag_in, outer_sin, precision=highest
    )
    imag_mid = jnp.einsum("...pq,pk->...kq", imag_in, outer_cos, precision=highest) - jnp.einsum(
        "...pq,pk->...kq", real_in, outer_sin, precision=highest
    )
    twist_cos, twist_sin = angle_table(outer_size, inner_size, length)
    real_twist = real_mid * twist_cos + imag_mid * twist_sin
    imag_twist = imag_mid * twist_cos - real_mid * twist_sin
    inner_cos, inner_sin = angle_table(inner_size, inner_size, inner_size)
    real_out = jnp.einsum("...kq,ql->...kl", real_twist, inner_cos, precision=highest) + jnp.einsum(
        "...kq,ql->...kl", imag_twist, inner_sin, precision=highest
    )
    imag_out = jnp.einsum("...kq,ql->...kl", imag_twist, inner_cos, precision=highest) - jnp.einsum(
        "...kq,ql->...kl", real_twist, inner_sin, precision=highest
    )
    real_out = jnp.swapaxes(real_out, -1, -2).reshape(leading + (length,))
    imag_out = jnp.swapaxes(imag_out, -1, -2).reshape(leading + (length,))
    return (real_out, imag_out)


def body(noise, elevation_library, tile_choice_index, family_heading_index, family_extent_index):
    line_count = noise.shape[1]
    side_cells = noise.shape[2]
    first_line = lax.axis_index(("row", "col")) * line_count
    v_index = first_line + lax.broadcasted_iota(jnp.int32, (line_count, side_cells), 0)
    u_index = lax.broadcasted_iota(jnp.int32, (line_count, side_cells), 1)
    amplitudes = amplitude(u_index, v_index, side_cells)
    real_part, imag_part = transform_last(noise[0] * amplitudes, noise[1] * amplitudes)
    spectrum = jnp.stack([real_part, imag_part])
    transposed = lax.all_to_all(
        spectrum.astype(jnp.bfloat16), ("row", "col"), split_axis=2, concat_axis=1, tiled=True
    ).astype(spectrum.dtype)
    turned = jnp.swapaxes(transposed, 1, 2)
    field_re, field_im = transform_last(turned[0], turned[1])
    fields = lax.all_to_all(
        jnp.stack([field_re, field_im]).astype(jnp.bfloat16),
        "col",
        split_axis=2,
        concat_axis=1,
        tiled=True,
    ).astype(jnp.float32)
    window_rows = fields.shape[1]
    window_columns = fields.shape[2]
    elevation_tiles = jnp.take(elevation_library, tile_choice_index, axis=0)
    slope_tangents = elevation_tiles.transpose(0, 2, 1, 3).reshape(window_rows, window_columns)
    secant = jnp.sqrt(1.0 + slope_tangents * slope_tangents)
    cohesion = 0.5 * jnp.exp(0.4 * fields[0])
    friction = 0.6 * jnp.exp(0.25 * fields[1])
    column_terms = jnp.stack(
        [cohesion * secant, friction / secant, slope_tangents / secant]
    ).astype(jnp.bfloat16)
    padded = extended(column_terms, (("row", 1), ("col", 2)), R)
    tile_width = min(128, window_columns)
    tile_count = window_columns // tile_width
    strip_span = tile_width + 2 * R
    strips = jnp.stack(
        [
            padded[:, :, tile_index * tile_width : tile_index * tile_width + strip_span]
            for tile_index in range(tile_count)
        ],
        axis=2,
    )
    kernel_width = 2 * R + 1
    shift_index = lax.broadcasted_iota(jnp.int32, (kernel_width, strip_span, tile_width), 0)
    strip_index = lax.broadcasted_iota(jnp.int32, (kernel_width, strip_span, tile_width), 1)
    out_index = lax.broadcasted_iota(jnp.int32, (kernel_width, strip_span, tile_width), 2)
    column_gap = strip_index - out_index
    offset_u = (shift_index - R).astype(jnp.float32)
    offset_v = (column_gap - R).astype(jnp.float32)
    inside_band = (column_gap >= 0) & (column_gap <= 2 * R)
    height, base_share = ellipsoid(
        offset_u[None],
        offset_v[None],
        family_heading_index[:, None, None, None],
        family_extent_index[:, None, None, None],
    )
    band_height = jnp.where(inside_band[None], height, 0.0).astype(jnp.bfloat16)
    band_share = jnp.where(inside_band[None], base_share, 0.0).astype(jnp.bfloat16)
    shifted = jnp.stack(
        [strips[:, row_shift : row_shift + window_rows] for row_shift in range(kernel_width)],
        axis=1,
    )
    resist_kernel = jnp.stack([band_share, band_height])
    resisting = jnp.einsum(
        "csxti,cfsio->fxto", shifted[0:2], resist_kernel, preferred_element_type=jnp.float32
    )
    driving = jnp.einsum(
        "sxti,fsio->fxto", shifted[2], band_height, preferred_element_type=jnp.float32
    )
    safety = resisting / driving
    family_low = jnp.min(safety, axis=0).reshape(window_rows, window_columns)
    half_width = window_columns // 2
    side_index = lax.axis_index("orient")
    own_half = lax.dynamic_slice_in_dim(family_low, side_index * half_width, half_width, 1)
    other_half = lax.dynamic_slice_in_dim(family_low, (1 - side_index) * half_width, half_width, 1)
    partner_half = partner(other_half, "orient", 0)
    return jnp.minimum(own_half, partner_half)


def solution(mesh):
    placed = (P(None, ("row", "col"), None), P(), P("row", "col"), P("orient"), P("orient"))
    return jax.shard_map(
        body, mesh=mesh, in_specs=placed, out_specs=P("row", ("col", "orient")), check_vma=False
    )
```

profile of v0, /device:TPU:13, one launch (start us, length us, event | category | flops | bytes accessed | tf_op | source)
XLA Modules:
  0.0 700.1 jit_solution(4212948183642729390)
XLA Ops:
  33.5 7.1 %fusion.40 = f32[256,32,128]{0,2,1:T(8,128)S(1)} fusion(f32[256,32,128]{2,1,0:T(8,128)S(1)} %get-tuple-element.8), kind=kOutput, calls=%fused_computation.91 | convolution fusion | flops 1610842112 | bytes 8388608 | tf_op jit(solution)/shard_map/...kq,ql->...kl/dot_general | solution.py:95
  48.5 6.8 fusion.61
  56.8 25.5 %copy.105 = bf16[2,256,4096]{1,0,2:T(2,128)(2,1)S(1)} copy(bf16[2,256,4096]{1,2,0:T(8,128)(2,1)S(1)} %pad_maximum_fusion.2) | data formatting | bytes 8388608 | tf_op jit(solution)/shard_map/stack | solution.py:111
  82.3 98.6 %all_to_all.27 = bf16[2,256,4096]{1,0,2:T(2,128)(2,1)S(1)} all-to-all(bf16[2,256,4096]{1,0,2:T(2,128)(2,1)S(1)} %copy.105), channel_id=1, replica_groups=mesh['row'=2,'col'=8,'orient'=2] {'row','col'}, dimensions={2} | all-to-all | bytes 8388608 | tf_op jit(solution)/shard_map/all_to_all | solution.py:112
  215.1 6.8 fusion.34
  222.0 6.8 fusion.32
  228.7 7.2 %fusion.62 = bf16[256,128,32]{0,1,2:T(8,128)(2,1)S(1)} fusion(f32[256,32,128]{0,2,1:T(8,128)S(1)} %fusion.34, f32[256,32,128]{2,1,0:T(8,128)S(1)} %get-tuple-element.5), kind=kOutput, calls=%fused_computation.116 | convolution fusion | flops 1612939264 | bytes 10485760 | tf_op jit(solution)/shard_map/...kq,ql->...kl/dot_general | solution.py:92
  237.1 6.7 fusion.63
  245.5 27.2 %copy.116 = bf16[2,256,4096]{1,0,2:T(2,128)(2,1)} copy(bf16[2,256,4096]{1,2,0:T(8,128)(2,1)S(1)} %pad_maximum_fusion.3) | data formatting | bytes 8388608 | tf_op jit(solution)/shard_map/stack | solution.py:118
  297.7 71.0 %all-to-all-done.1 = bf16[2,256,4096]{1,0,2:T(2,128)(2,1)} async-done(((bf16[2,256,4096]{1,0,2:T(2,128)(2,1)}), bf16[2,256,4096]{1,0,2:T(2,128)(2,1)}, u32[]{:S(2)}, u32[]{:S(2)}) %all-to-all-start.1) | async-done | bytes 4194336 | tf_op jit(solution)/shard_map/all_to_all | solution.py:117
  405.0 12.7 %concatenate.10 = bf16[3,2064,512]{1,2,0:T(8,128)(2,1)} concatenate(bf16[3,8,512]{1,2,0:T(8,128)(2,1)} %copy-done.11, bf16[3,2048,512]{1,2,0:T(8,128)(2,1)} %copy-done.2, bf16[3,8,512]{1,2,0:T(8,128)(2,1)} %collective-permute-done.1), dimensions={1} | concatenate | bytes 12681216 | tf_op jit(solution)/shard_map/concatenate | solution.py:24
  440.5 6.7 fusion.18
  460.6 6.9 fusion.15
  467.4 6.7 fusion.14
  480.9 6.9 fusion.12
  494.5 6.7 fusion.10
  501.2 7.0 %fusion.9 = bf16[3,17,2048,4,144]{2,4,1,0,3:T(8,128)(2,1)} fusion(bf16[3,17,2048,4,144]{2,4,1,0,3:T(8,128)(2,1)} %fusion.10, bf16[3,2064,4,144]{1,3,0,2:T(8,128)(2,1)S(1)} %pad_maximum_fusion), kind=kLoop, calls=%fused_computation.22 | loop fusion | bytes 14155776
  508.2 6.7 fusion.8
  521.6 6.8 fusion.6
  528.4 6.7 fusion.5
  535.1 6.7 fusion.4
  548.6 51.8 %fusion = f32[4,128,2048,4,1,1]{2,1,5,4,3,0:T(8,128)} fusion(bf16[3,17,2048,4,144]{2,4,1,0,3:T(8,128)(2,1)} %fusion.3, bf16[2,4,17,144,128,1]{4,3,2,0,5,1:T(8,128)(2,1)} %maximum_bitcast_fusion.4), kind=kOutput, calls=%fused_computation.2 | convolution fusion | flops 41070624768 | bytes 102006784 | tf_op jit(solution)/shard_map/csxti,cfsio->fxto/dot_general | solution.py:166
  600.5 42.4 %fusion.2 = f32[128,2048,4]{1,0,2:T(8,128)} fusion(f32[4,128,2048,4,1,1]{2,1,5,4,3,0:T(8,128)} %fusion, bf16[3,17,2048,4,144]{2,4,1,0,3:T(8,128)(2,1)} %fusion.3, f32[4]{0:T(128)S(1)} %copy-done.16, f32[4]{0:T(128)S(1)} %copy-done.14, f32[4]{0:T(128)S(1)} %copy-done.20, f32[17,144,128]{2,1,0:T(8,128)S(1)} %copy-done.8, f32[4]{0:T(128)S(1)} %copy-done.22, ...), kind=kOutput, calls=%fused_computation.6 | convolution fusion | flops 20562706432 | bytes 62646420 | tf_op jit(solution)/shard_map/sxti,fsio->fxto/dot_general | solution.py:169
  652.7 43.4 %collective-permute-done.4 = f32[2048,256]{1,0:T(8,128)} collective-permute-done((f32[2048,256]{1,0:T(8,128)}, f32[2048,256]{1,0:T(8,128)}, u32[]{:S(2)}, u32[]{:S(2)}) %collective-permute-start.4) | collective-permute-done | bytes 2097184 | tf_op jit(solution)/shard_map/ppermute | solution.py:36
  (129 shorter events, 217.3 us)
Async XLA Ops:
  0.0 278.3 %copy-start = (f32[16,128,128]{2,1,0:T(8,128)S(1)}, f32[16,128,128]{2,1,0:T(8,128)}, u32[]{:S(2)}) copy-start(f32[16,128,128]{2,1,0:T(8,128)} %param.6) | copy-start | bytes 3145732
  272.7 96.0 %all-to-all-start.1 = ((bf16[2,256,4096]{1,0,2:T(2,128)(2,1)}), bf16[2,256,4096]{1,0,2:T(2,128)(2,1)}, u32[]{:S(2)}, u32[]{:S(2)}) async-start(bf16[2,256,4096]{1,0,2:T(2,128)(2,1)} %copy.116), calls=%async_computation.1 | async-start | bytes 8388608 | tf_op jit(solution)/shard_map/all_to_all | solution.py:117
  296.2 101.8 %copy-start.23 = (f32[17]{0:T(128)}, f32[17]{0:T(128)S(1)}, u32[]{:S(2)}) copy-start(f32[17]{0:T(128)S(1)} %add_convert_fusion.3) | copy-start | bytes 208
  296.3 101.7 %copy-start.9 = (pred[17,144,128]{2,1,0:T(8,128)(4,1)}, pred[17,144,128]{2,1,0:T(8,128)(4,1)S(1)}, u32[]{:S(2)}) copy-start(pred[17,144,128]{2,1,0:T(8,128)(4,1)S(1)} %fusion.76) | copy-start | bytes 940036
  297.6 100.4 %copy-start.13 = (f32[4]{0:T(128)}, f32[4]{0:T(128)S(1)}, u32[]{:S(2)}) copy-start(f32[4]{0:T(128)S(1)} %get-tuple-element.34) | copy-start | bytes 52
  297.6 100.4 %copy-start.15 = (f32[4]{0:T(128)}, f32[4]{0:T(128)S(1)}, u32[]{:S(2)}) copy-start(f32[4]{0:T(128)S(1)} %get-tuple-element.35) | copy-start | bytes 52
  297.6 100.4 %copy-start.17 = (f32[4]{0:T(128)}, f32[4]{0:T(128)S(1)}, u32[]{:S(2)}) copy-start(f32[4]{0:T(128)S(1)} %get-tuple-element.36) | copy-start | bytes 52
  297.6 100.4 %copy-start.19 = (f32[4]{0:T(128)}, f32[4]{0:T(128)S(1)}, u32[]{:S(2)}) copy-start(f32[4]{0:T(128)S(1)} %get-tuple-element.39) | copy-start | bytes 52
  297.7 100.4 %copy-start.21 = (f32[4]{0:T(128)}, f32[4]{0:T(128)S(1)}, u32[]{:S(2)}) copy-start(f32[4]{0:T(128)S(1)} %get-tuple-element.40) | copy-start | bytes 52
  385.3 12.8 %copy-start.7 = (f32[17,144,128]{2,1,0:T(8,128)S(1)}, f32[17,144,128]{2,1,0:T(8,128)}, u32[]{:S(2)}) copy-start(f32[17,144,128]{2,1,0:T(8,128)} %add_convert_fusion.2) | copy-start | bytes 3760132
  392.0 12.1 %collective-permute-start = (bf16[3,8,512]{1,2,0:T(8,128)(2,1)S(1)}, bf16[3,8,512]{1,2,0:T(8,128)(2,1)S(1)}, u32[]{:S(2)}, u32[]{:S(2)}) collective-permute-start(bf16[3,8,512]{1,2,0:T(8,128)(2,1)S(1)} %get-tuple-element.20), channel_id=1, source_target_pairs={{0,16},{1,17},{2,18},{3,19},{4,20},{5,21},{6,22},{7,23},{8,24},{9,... | collective-permute-start | bytes 73736 | tf_op jit(solution)/shard_map/ppermute | solution.py:26
  393.3 11.7 %collective-permute-start.1 = (bf16[3,8,512]{1,2,0:T(8,128)(2,1)S(1)}, bf16[3,8,512]{1,2,0:T(8,128)(2,1)}, u32[]{:S(2)}, u32[]{:S(2)}) collective-permute-start(bf16[3,8,512]{1,2,0:T(8,128)(2,1)S(1)} %get-tuple-element.19), channel_id=1, source_target_pairs={{16,0},{17,1},{18,2},{19,3},{20,4},{21,5},{22,6},{23,7},{24,8},{25... | collective-permute-start | bytes 73736 | tf_op jit(solution)/shard_map/ppermute | solution.py:28
  418.7 10.5 %collective-permute-start.2 = (bf16[3,2064,8]{1,2,0:T(8,128)(2,1)S(1)}, bf16[3,2064,8]{1,2,0:T(8,128)(2,1)S(1)}, u32[]{:S(2)}, u32[]{:S(2)}) collective-permute-start(bf16[3,2064,8]{1,2,0:T(8,128)(2,1)S(1)} %get-tuple-element.17), channel_id=1, source_target_pairs={{0,2},{2,4},{4,6},{6,8},{8,10},{10,12},{12,14},{1,3},{3,5},{5,7},{... | collective-permute-start | bytes 297224 | tf_op jit(solution)/shard_map/ppermute | solution.py:26
  422.9 6.3 collective-permute-start.3
  548.5 51.9 %copy-start.8 = (f32[17,144,128]{2,1,0:T(8,128)S(1)}, f32[17,144,128]{2,1,0:T(8,128)}, u32[]{:S(2)}) copy-start(f32[17,144,128]{2,1,0:T(8,128)} %add_convert_fusion.2) | copy-start | bytes 3760132
  548.5 51.9 %copy-start.10 = (pred[17,144,128]{2,1,0:T(8,128)(4,1)S(1)}, pred[17,144,128]{2,1,0:T(8,128)(4,1)}, u32[]{:S(2)}) copy-start(pred[17,144,128]{2,1,0:T(8,128)(4,1)} %copy-done.9) | copy-start | bytes 940036
  548.5 51.9 %copy-start.14 = (f32[4]{0:T(128)S(1)}, f32[4]{0:T(128)}, u32[]{:S(2)}) copy-start(f32[4]{0:T(128)} %copy-done.13) | copy-start | bytes 52
  548.5 51.9 %copy-start.16 = (f32[4]{0:T(128)S(1)}, f32[4]{0:T(128)}, u32[]{:S(2)}) copy-start(f32[4]{0:T(128)} %copy-done.15) | copy-start | bytes 52
  548.5 51.9 %copy-start.18 = (f32[4]{0:T(128)S(1)}, f32[4]{0:T(128)}, u32[]{:S(2)}) copy-start(f32[4]{0:T(128)} %copy-done.17) | copy-start | bytes 52
  548.5 51.9 %copy-start.20 = (f32[4]{0:T(128)S(1)}, f32[4]{0:T(128)}, u32[]{:S(2)}) copy-start(f32[4]{0:T(128)} %copy-done.19) | copy-start | bytes 52
  548.5 51.9 %copy-start.22 = (f32[4]{0:T(128)S(1)}, f32[4]{0:T(128)}, u32[]{:S(2)}) copy-start(f32[4]{0:T(128)} %copy-done.21) | copy-start | bytes 52
  548.6 51.9 %copy-start.24 = (f32[17]{0:T(128)S(1)}, f32[17]{0:T(128)}, u32[]{:S(2)}) copy-start(f32[17]{0:T(128)} %copy-done.23) | copy-start | bytes 208
  649.7 46.4 %collective-permute-start.4 = (f32[2048,256]{1,0:T(8,128)}, f32[2048,256]{1,0:T(8,128)}, u32[]{:S(2)}, u32[]{:S(2)}) collective-permute-start(f32[2048,256]{1,0:T(8,128)} %copy.147), channel_id=1, source_target_pairs={{0,1},{1,0},{2,3},{3,2},{4,5},{5,4},{6,7},{7,6},{8,9},{9,8},{10,11... | collective-permute-start | bytes 6291464 | tf_op jit(solution)/shard_map/ppermute | solution.py:36
  650.9 49.0 %copy-start.1 = (f32[16,128,128]{2,1,0:T(8,128)S(1)}, f32[16,128,128]{2,1,0:T(8,128)}, u32[]{:S(2)}) copy-start(f32[16,128,128]{2,1,0:T(8,128)} %param.6) | copy-start | bytes 3145732
  (9 other events, 33.4 us)
where the time goes:
time: 711 us; the launch traced here: 700 us
  local copies, waits for them, and re-layouts  243 us (34%)
  matrix products  178 us (25%)
  waiting for transfers between devices  115 us (16%)
  blocking collectives  98.6 us (14%)
  other arithmetic  45.2 us (6%)
  starting transfers between devices  18.8 us (3%)
    unnamed x75, local copies, waits for them, and re-layouts  122 us
    all_to_all x1, blocking collectives, body(): lax.all_to_all(spectrum.astype(jnp.bfloat16), ('row', 'col'), split_axis=...  98.6 us
    all_to_all x1, waiting for transfers between devices, body(): lax.all_to_all(jnp.stack([field_re, field_im]).astype(jnp.bfloat16), 'col...  71 us
    dot_general x1, matrix products, body(): jnp.einsum('csxti,cfsio->fxto', shifted[0:2], resist_kernel, preferred_el...  51.8 us
    ppermute x1, waiting for transfers between devices, partner(): lax.ppermute(x, axis, [(i, i ^ 1 << bit) for i in range(lax.axis_size(axi...  43.4 us
    dot_general x1, matrix products, body(): jnp.einsum('sxti,fsio->fxto', shifted[2], band_height, preferred_element_...  42.4 us
    another operation x1, local copies, waits for them, and re-layouts, body(): jnp.stack([field_re, field_im]).astype(jnp.bfloat16)  27.2 us
    another operation x1, local copies, waits for them, and re-layouts, body(): spectrum = jnp.stack([real_part, imag_part])  25.5 us
  transfers between devices with their start and end apart: 6, of which 4 were waited for; matrix products, arithmetic and copies ran while one was open for 4% of the time, Pallas kernels for 0%

commit v1 on v0

v1 whole, which is shorter than its diff:
```python
import functools
import math

import jax
import jax.numpy as jnp
import numpy as np
from jax import lax
from jax.experimental import pallas as pl
from jax.experimental.pallas import tpu as pltpu
from jax.sharding import PartitionSpec as P

R = 8
N_AZ = 36
NSIZE = 4
LANES = 128
TILE_ROWS = 8
TILE_LANES = 16
GROUPS = LANES // TILE_LANES
PHASE = TILE_ROWS * TILE_LANES

nugget_share = 0.3
peak_share = 1024.0 / (2.0 * math.pi)
cutoff_ratio = 32.0


def amplitude(u_index, v_index, side_cells):
    wrap_u = jnp.minimum(u_index, side_cells - u_index).astype(jnp.float32)
    wrap_v = jnp.minimum(v_index, side_cells - v_index).astype(jnp.float32)
    cutoff = side_cells / cutoff_ratio
    scaled_u = wrap_u / cutoff
    scaled_v = wrap_v / cutoff
    grown = 1.0 + scaled_u * scaled_u + scaled_v * scaled_v
    spectrum = nugget_share + peak_share / (grown * jnp.sqrt(grown))
    return jnp.sqrt(spectrum) / side_cells


def ellipsoid(offset_u, offset_v, azimuth, size_index):
    heading = azimuth.astype(jnp.float32) * (math.pi / N_AZ)
    semi_axis = R * (size_index.astype(jnp.float32) + (1 + NSIZE)) / (2 * NSIZE)
    across = 0.6 * semi_axis
    slip_depth = 0.3 * semi_axis
    along = offset_u * jnp.cos(heading) + offset_v * jnp.sin(heading)
    lateral = offset_v * jnp.cos(heading) - offset_u * jnp.sin(heading)
    along_part = along / semi_axis
    lateral_part = lateral / across
    inside = 1.0 - along_part * along_part - lateral_part * lateral_part
    height = slip_depth * jnp.sqrt(jnp.maximum(inside, 0.0))
    base_share = jnp.clip(4.0 * inside, 0.0, 1.0)
    return (height, base_share)


def small_dft(parts):
    count = len(parts)
    if count == 1:
        return parts
    even = small_dft(parts[0::2])
    odd = small_dft(parts[1::2])
    low, high = [], []
    for k in range(count // 2):
        (a, b), (c, d) = even[k], odd[k]
        if k == 0:
            e, f = c, d
        elif 4 * k == count:
            e, f = d, -c
        else:
            cos = math.cos(2 * math.pi * k / count)
            sin = math.sin(2 * math.pi * k / count)
            e, f = c * cos + d * sin, d * cos - c * sin
        low.append((a + e, b + f))
        high.append((a - e, b - f))
    return low + high


def transform_kernel(planes, blocks, span, step, pad, in_ref, cos_ref, sin_ref, big_ref, small_ref, out_ref, mid, full):
    outer = cos_ref.shape[0]
    rows = mid.shape[1]
    unit = 16 if planes else 8

    @pl.loop(0, rows // unit)
    def _(block):
        at = pl.ds(pl.multiple_of(block * unit, unit), unit)
        parts = []
        for p in range(outer):
            if planes:
                parts.append((in_ref[p, 0, at, :].astype(jnp.float32), in_ref[p, 1, at, :].astype(jnp.float32)))
            else:
                lanes = slice(p * LANES, (p + 1) * LANES)
                parts.append((in_ref[0, at, lanes], in_ref[1, at, lanes]))
        for k, (re, im) in enumerate(small_dft(parts)):
            cos = cos_ref[k : k + 1, :]
            sin = sin_ref[k : k + 1, :]
            mid[k, at, 0:LANES] = re * cos + im * sin
            mid[k, at, LANES : 2 * LANES] = im * cos - re * sin

    if pad:
        edge = jnp.zeros((pad, rows), jnp.float32)
        for part in range(2):
            full[part, 0:pad, :] = edge
            full[part, pad + outer * LANES : 2 * pad + outer * LANES, :] = edge

    turned = (((1,), (1,)), ((), ()))
    dot = functools.partial(lax.dot_general, dimension_numbers=turned, preferred_element_type=jnp.float32)
    for k in range(outer):
        value = mid[k]
        high = value.astype(jnp.bfloat16)
        rest = (value - high.astype(jnp.float32)).astype(jnp.bfloat16)
        got = dot(big_ref[...], high) + dot(big_ref[...], rest) + dot(small_ref[...], high)
        full[0, pl.ds(pad + k, LANES, stride=outer), :] = got[0:LANES]
        full[1, pl.ds(pad + k, LANES, stride=outer), :] = got[LANES : 2 * LANES]

    @pl.loop(0, blocks)
    def _(block):
        at = pl.ds(pl.multiple_of(block * step, 8), span)
        for part in range(2):
            out_ref[block, part] = full[part, at, :].astype(jnp.bfloat16)


def transform(cells, planes, rows, length, blocks, pad):
    outer = length // LANES
    step = length // blocks
    span = step + 2 * pad
    k = np.arange(outer)[:, None]
    q = np.arange(LANES)
    turn = 2 * np.pi * k * q / length
    cos, sin = np.cos(turn).astype(np.float32), np.sin(turn).astype(np.float32)
    angle = 2 * np.pi * (q[:, None] * q % LANES) / LANES
    table = np.block([[np.cos(angle), np.sin(angle)], [-np.sin(angle), np.cos(angle)]]).astype(np.float32)
    big = table.astype(jnp.bfloat16)
    small = (table - big.astype(np.float32)).astype(jnp.bfloat16)
    vmem = pl.BlockSpec(memory_space=pltpu.VMEM)
    return pl.pallas_call(
        functools.partial(transform_kernel, planes, blocks, span, step, pad),
        out_shape=jax.ShapeDtypeStruct((blocks, 2, span, rows), jnp.bfloat16),
        in_specs=[vmem] * 5,
        out_specs=vmem,
        scratch_shapes=[
            pltpu.VMEM((outer, rows, 2 * LANES), jnp.float32),
            pltpu.VMEM((2, length + 2 * pad, rows), jnp.float32),
        ],
        compiler_params=pltpu.CompilerParams(vmem_limit_bytes=40 << 20),
    )(cells, cos, sin, big, small)


def swap_groups(cells):
    row = lax.broadcasted_iota(jnp.int32, cells.shape, 1)
    group = lax.broadcasted_iota(jnp.int32, cells.shape, 2) // TILE_LANES
    for bit in (4, 2, 1):
        row_set = (row & bit) != 0
        group_set = (group & bit) != 0
        lane = bit * TILE_LANES
        down = pltpu.roll(pltpu.roll(cells, TILE_ROWS - bit, 1), lane, 2)
        up = down if bit == 4 else pltpu.roll(pltpu.roll(cells, bit, 1), LANES - lane, 2)
        cells = jnp.where(row_set == group_set, cells, jnp.where(group_set, down, up))
    return cells


def stability_kernel(families, term_ref, band_ref, out_ref, swapped, gathered):
    tiles = gathered.shape[1]
    across = gathered.shape[2]
    chunks = across // GROUPS

    @pl.when(pl.program_id(0) == 0)
    def _():
        @pl.loop(0, tiles // 2)
        def _(pair):
            at = pl.ds(pl.multiple_of(pair * 16, 16), 16)
            for term in range(3):
                for chunk in range(chunks + 1):
                    cells = term_ref[term, at, chunk * LANES : (chunk + 1) * LANES].astype(jnp.float32)
                    turned = swap_groups(cells.reshape(2, TILE_ROWS, LANES))
                    swapped[:, chunk * GROUPS : (chunk + 1) * GROUPS, :] = turned
                both = pl.ds(pair * 2, 2)
                gathered[term, both, :, 0:PHASE] = swapped[:, 0:across, :].astype(jnp.bfloat16)
                gathered[term, both, :, PHASE:] = swapped[:, 1 : across + 1, :].astype(jnp.bfloat16)

    tile = pl.program_id(0) * 2
    low = None
    for pair in range(families // 2):
        lanes = slice(pair * 2 * PHASE, (pair + 1) * 2 * PHASE)
        resisting = driving = None
        for shift in range(3):
            for term in range(3):
                left = gathered[term, pl.ds(tile + shift, 2)].reshape(2 * across, 2 * PHASE)
                got = jnp.dot(left, band_ref[term, shift, :, lanes], preferred_element_type=jnp.float32)
                if term == 2:
                    driving = got if driving is None else driving + got
                else:
                    resisting = got if resisting is None else resisting + got
        ratio = resisting / driving
        least = jnp.minimum(ratio[:, 0:PHASE], ratio[:, PHASE:])
        low = least if low is None else jnp.minimum(low, least)
    turned = swap_groups(low.reshape(2 * chunks, TILE_ROWS, LANES))
    for side in range(2):
        for chunk in range(chunks):
            out_ref[side * 8 : side * 8 + 8, chunk * LANES : (chunk + 1) * LANES] = turned[side * chunks + chunk]


def stability(terms, band, height, width):
    families = band.shape[-1] // PHASE
    across = width // TILE_LANES
    tiles = height // TILE_ROWS + 2
    return pl.pallas_call(
        functools.partial(stability_kernel, families),
        grid=(height // 16,),
        out_shape=jax.ShapeDtypeStruct((height, width), jnp.float32),
        in_specs=[
            pl.BlockSpec(terms.shape, lambda i: (0, 0, 0), pipeline_mode=pl.Buffered(1)),
            pl.BlockSpec(band.shape, lambda i: (0, 0, 0, 0), pipeline_mode=pl.Buffered(1)),
        ],
        out_specs=pl.BlockSpec((16, width), lambda i: (i, 0)),
        scratch_shapes=[
            pltpu.VMEM((2, across + GROUPS, LANES), jnp.float32),
            pltpu.VMEM((3, tiles, across, 2 * PHASE), jnp.bfloat16),
        ],
        compiler_params=pltpu.CompilerParams(vmem_limit_bytes=48 << 20),
    )(terms, band)


def band_weights(headings, extents):
    shape = (3, 2, TILE_ROWS, TILE_LANES, TILE_ROWS, TILE_LANES)
    index = [lax.broadcasted_iota(jnp.int32, shape, axis) for axis in range(6)]
    offset_v = TILE_ROWS * index[0] + index[2] - R - index[4]
    offset_u = TILE_LANES * index[1] + index[3] - R - index[5]
    keep = (jnp.abs(offset_v) <= R) & (jnp.abs(offset_u) <= R)
    rows = 3 * 2 * PHASE

    def flat(cells):
        return cells.reshape(rows, 1, PHASE)

    heights, shares = ellipsoid(
        flat(offset_u.astype(jnp.float32)),
        flat(offset_v.astype(jnp.float32)),
        headings[None, :, None],
        extents[None, :, None],
    )
    keep = flat(keep)
    count = headings.shape[0]

    def whole(cells):
        return jnp.where(keep, cells, 0.0).astype(jnp.bfloat16).reshape(3, 2 * PHASE, count * PHASE)

    heights = whole(heights)
    return jnp.stack([whole(shares), heights, heights])


def body(noise, elevation_library, tile_choice_index, family_heading_index, family_extent_index):
    side_cells = noise.shape[2]
    row_count = lax.axis_size("row")
    col_count = lax.axis_size("col")
    split = lax.axis_size("orient")
    row, col, side = (lax.axis_index(axis) for axis in ("row", "col", "orient"))
    devices = row_count * col_count * split
    lines = noise.shape[1] // split
    window_rows = side_cells // row_count
    window_columns = side_cells // (col_count * split)

    families = lax.all_gather(
        jnp.stack([family_heading_index, family_extent_index]), "orient", axis=1, tiled=True
    )
    choices = lax.all_gather(tile_choice_index, "row", axis=0, tiled=True)
    choices = lax.all_gather(choices, "col", axis=1, tiled=True)

    own = lax.dynamic_slice_in_dim(noise, side * lines, lines, 1)
    first_line = lax.axis_index(("row", "col", "orient")) * lines
    v_index = first_line + lax.broadcasted_iota(jnp.int32, (lines, side_cells), 0)
    u_index = lax.broadcasted_iota(jnp.int32, (lines, side_cells), 1)
    weights = own * amplitude(u_index, v_index, side_cells)[None]
    spectrum = transform(weights, False, lines, side_cells, devices, 0)
    held = lax.all_to_all(spectrum, ("row", "col", "orient"), split_axis=0, concat_axis=0, tiled=True)
    positions = side_cells // devices
    per_block = LANES // lines
    held = held.reshape(side_cells // LANES, per_block, 2, positions, lines)
    held = held.transpose(0, 2, 3, 1, 4).reshape(side_cells // LANES, 2, positions, LANES)
    fields = transform(held, True, positions, side_cells, col_count * split, R)
    fields = lax.all_to_all(fields, ("col", "orient"), split_axis=0, concat_axis=0, tiled=True)
    tall = window_columns + 2 * R
    fields = fields.transpose(1, 2, 0, 3).reshape(2, tall, window_rows)
    ends = row_count - 1
    before = lax.ppermute(fields[:, :, window_rows - R :], "row", [(i, i + 1) for i in range(ends)])
    after = lax.ppermute(fields[:, :, :R], "row", [(i + 1, i) for i in range(ends)])
    wide = (window_rows // LANES + 1) * LANES
    spare = wide - window_rows - 2 * R
    fields = jnp.concatenate(
        [before, fields, after, jnp.zeros((2, tall, spare), fields.dtype)], axis=2
    ).astype(jnp.float32)

    tile_side = elevation_library.shape[1]
    tiles_x = window_rows // tile_side
    tiles_y = window_columns // tile_side
    first_y = col * split + side
    padded_choices = jnp.pad(choices, 1)
    local = lax.dynamic_slice(
        padded_choices, (row * tiles_x, first_y * tiles_y), (tiles_x + 2, tiles_y + 2)
    )
    slope = jnp.take(elevation_library.transpose(0, 2, 1), local.T, axis=0, mode="clip")
    slope = slope.transpose(0, 2, 1, 3).reshape((tiles_y + 2) * tile_side, (tiles_x + 2) * tile_side)
    edge = tile_side - R
    slope = slope[edge : edge + tall, edge : edge + wide]
    y = first_y * window_columns - R + lax.broadcasted_iota(jnp.int32, (tall, wide), 0)
    x = row * window_rows - R + lax.broadcasted_iota(jnp.int32, (tall, wide), 1)
    inside = (y >= 0) & (y < side_cells) & (x >= 0) & (x < side_cells)
    secant = jnp.sqrt(1.0 + slope * slope)
    cohesion = 0.5 * jnp.exp(0.4 * fields[0])
    friction = 0.6 * jnp.exp(0.25 * fields[1])
    terms = jnp.stack([cohesion * secant, friction / secant, slope / secant])
    terms = jnp.where(inside[None], terms, 0.0).astype(jnp.bfloat16)
    band = band_weights(families[0], families[1])
    return stability(terms, band, window_columns, window_rows).T


def solution(mesh):
    placed = (P(None, ("row", "col"), None), P(), P("row", "col"), P("orient"), P("orient"))
    return jax.shard_map(
        body, mesh=mesh, in_specs=placed, out_specs=P("row", ("col", "orient")), check_vma=False
    )
```

time: 711 us -> 254 us (0.36); the launches traced: 700 us -> 253 us
  local copies, waits for them, and re-layouts: 243 us -> 42.1 us
  matrix products: 178 us -> 0 us
  Pallas kernels: 0 us -> 93.3 us
  waiting for transfers between devices: 115 us -> 26.9 us
  blocking collectives: 98.6 us -> 48.4 us
  other arithmetic: 45.2 us -> 22.2 us
    dot_general x18 -> x0, matrix products: 178 us -> none  [the longest x1 51.8 us: body(): jnp.einsum('csxti,cfsio->fxto', shifted[0:2], resist_kernel, preferred_el...]
    unnamed x75 -> x34, local copies, waits for them, and re-layouts: 122 us -> 4.55 us
    all_to_all x1 -> x0, blocking collectives: 98.6 us -> none  [body(): lax.all_to_all(spectrum.astype(jnp.bfloat16), ('row', 'col'), split_axis=...]
    pallas_call x0 -> x3, Pallas kernels: none -> 93.3 us  [the longest x1 75.7 us: stability(): pl.pallas_call(functools.partial(stability_kernel, families), grid=(heigh...]
    another operation x5 -> x0, local copies, waits for them, and re-layouts: 67.6 us -> none  [the longest x1 27.2 us: body(): jnp.stack([field_re, field_im]).astype(jnp.bfloat16)]
    all_gather x0 -> x3, blocking collectives: none -> 48.4 us  [the longest x1 32.8 us: body(): choices = lax.all_gather(choices, 'col', axis=1, tiled=True)]
    all_to_all x1 -> x2, waiting for transfers between devices: 71 us -> 26.9 us  [the longest x1 26.9 us: body(): lax.all_to_all(fields, ('col', 'orient'), split_axis=0, concat_axis=0, ti...]
    ppermute x5 -> x2, waiting for transfers between devices: 44 us -> 0.01 us  [the longest x1 0.01 us: body(): lax.ppermute(fields[:, :, window_rows - R:], 'row', [(i, i + 1) for i in...]
  transfers between devices with their start and end apart: 6 -> 4, of which waited for: 4 -> 1; matrix products, arithmetic and copies ran while one was open for 4% -> 18% of each run, Pallas kernels for 0% -> 0%
where the time goes in v1:
time: 254 us; the launch traced here: 253 us
  Pallas kernels  93.3 us (37%)
  blocking collectives  48.4 us (19%)
  local copies, waits for them, and re-layouts  42.1 us (17%)
  waiting for transfers between devices  26.9 us (11%)
  other arithmetic  22.2 us (9%)
  starting transfers between devices  19.9 us (8%)
    pallas_call x1, Pallas kernels, stability(): pl.pallas_call(functools.partial(stability_kernel, families), grid=(heigh...  75.7 us
    all_gather x1, blocking collectives, body(): choices = lax.all_gather(choices, 'col', axis=1, tiled=True)  32.8 us
    all_to_all x1, waiting for transfers between devices, body(): lax.all_to_all(fields, ('col', 'orient'), split_axis=0, concat_axis=0, ti...  26.9 us
    pallas_call x2, Pallas kernels, transform(): pl.pallas_call(functools.partial(transform_kernel, planes, blocks, span,...  17.6 us
    mul x5, local copies, waits for them, and re-layouts, ellipsoid(): along = offset_u * jnp.cos(heading) + offset_v * jnp.sin(heading)  13 us
    all_gather x1, blocking collectives, body(): lax.all_gather(jnp.stack([family_heading_index, family_extent_index]), 'o...  11.9 us
    gather x2, local copies, waits for them, and re-layouts, body(): jnp.take(elevation_library.transpose(0, 2, 1), local.T, axis=0, mode='clip')  8.83 us
    all_to_all x1, starting transfers between devices, body(): lax.all_to_all(fields, ('col', 'orient'), split_axis=0, concat_axis=0, ti...  8.37 us
  transfers between devices with their start and end apart: 4, of which 1 were waited for; matrix products, arithmetic and copies ran while one was open for 18% of the time, Pallas kernels for 0%

profile of v1, /device:TPU:13, one launch (start us, length us, event | category | flops | bytes accessed | tf_op | source)
XLA Modules:
  0.0 253.1 jit_solution(4068123326718178415)
XLA Ops:
  1.5 2.7 %dynamic-slice_multiply_fusion.in_ref = f32[2,128,4096]{2,1,0:T(8,128)S(1)} fusion(f32[2,256,4096]{2,1,0:T(8,128)} %param.13, s32[]{:T(128)S(6)} %select_n.34, f32[128,4096]{1,0:T(8,128)S(1)} %fusion.14), kind=kLoop, calls=%fused_computation.5 | loop fusion | flops 1048576 | bytes 10485764 | tf_op jit(solution)/shard_map/mul | solution.py:267
  4.3 8.6 %shard_map.127 = bf16[32,2,128,128]{3,2,1,0:T(8,128)(2,1)} custom-call(f32[2,128,4096]{2,1,0:T(8,128)S(1)} %dynamic-slice_multiply_fusion.in_ref, f32[32,128]{1,0:T(8,128)S(1)} %copy-done.4, f32[32,128]{1,0:T(8,128)S(1)} %copy-done.5, bf16[256,256]{1,0:T(8,128)(2,1)S(1)} %copy-done.2, bf16[256,256]{1,0:T(8,128)(2,1)S(1)} %copy-done.3), custom_call_target="tpu_custom_call" | custom-call | tf_op jit(solution)/shard_map/pallas_call | solution.py:131
  12.9 6.3 %all-to-all-start = ((bf16[32,2,128,128]{3,2,1,0:T(8,128)(2,1)}), bf16[32,2,128,128]{3,2,1,0:T(8,128)(2,1)S(1)}, u32[]{:S(2)}, u32[]{:S(2)}) async-start(bf16[32,2,128,128]{3,2,1,0:T(8,128)(2,1)} %shard_map.127), calls=%async_computation | async-start | bytes 4194304 | tf_op jit(solution)/shard_map/all_to_all | solution.py:269
  19.2 11.9 %all-gather.2 = s32[2,4,2]{1,2,0:T(2,128)} all-gather(s32[1,4,2]{1,2,0:T(2,128)S(1)} %add_bitcast_fusion), channel_id=1, replica_groups=mesh['row'=2,'col'=8,'orient'=2] {'orient'}, dimensions={0}, use_global_device_ids=true | all-gather | bytes 96 | tf_op jit(solution)/shard_map/all_gather | solution.py:257
  31.1 3.7 %all-gather = s32[2,16,4]{1,2,0:T(4,128)S(1)} all-gather(s32[1,16,4]{1,2,0:T(4,128)S(1)} %bitcast.88), channel_id=1, replica_groups=mesh['row'=2,'col'=8,'orient'=2] {'row'}, dimensions={0}, use_global_device_ids=true | all-gather | bytes 768 | tf_op jit(solution)/shard_map/all_gather | solution.py:260
  37.6 32.8 %all-gather.1 = s32[8,4,32]{2,1,0:T(4,128)S(1)} all-gather(s32[1,4,32]{2,1,0:T(4,128)S(1)} %bitcast.85), channel_id=1, replica_groups=mesh['row'=2,'col'=8,'orient'=2] {'col'}, dimensions={0}, use_global_device_ids=true | all-gather | bytes 4608 | tf_op jit(solution)/shard_map/all_gather | solution.py:261
  73.0 9.0 %shard_map.128 = bf16[16,2,272,128]{3,2,1,0:T(8,128)(2,1)} custom-call(bf16[32,2,128,128]{3,2,1,0:T(8,128)(2,1)S(1)} %all-to-all-done.in_ref, f32[32,128]{1,0:T(8,128)S(1)} %copy-done.4, f32[32,128]{1,0:T(8,128)S(1)} %copy-done.5, bf16[256,256]{1,0:T(8,128)(2,1)S(1)} %copy-done.2, bf16[256,256]{1,0:T(8,128)(2,1)S(1)} %copy-done.3), custom_call_target="tpu_custom_call" | custom-call | tf_op jit(solution)/shard_map/pallas_call | solution.py:131
  82.0 8.4 %all-to-all-start.1 = ((bf16[16,2,272,128]{3,2,1,0:T(8,128)(2,1)}), bf16[16,2,272,128]{3,2,1,0:T(8,128)(2,1)}, u32[]{:S(2)}, u32[]{:S(2)}) async-start(bf16[16,2,272,128]{3,2,1,0:T(8,128)(2,1)} %shard_map.128), calls=%async_computation.1 | async-start | bytes 4456448 | tf_op jit(solution)/shard_map/all_to_all | solution.py:275
  94.3 4.6 %mul.334 = f32[1,3,256,1024]{3,2,1,0:T(8,128)} reshape(f32[768,8,128]{2,1,0:T(8,128)} %mul.333) | data formatting | bytes 6291456 | tf_op jit(solution)/shard_map/mul | solution.py:42
  99.1 1.9 mul.340
  101.0 4.5 %mul.341 = f32[1,3,256,1024]{3,2,1,0:T(8,128)} reshape(f32[768,8,128]{2,1,0:T(8,128)} %mul.340) | data formatting | bytes 6291456 | tf_op jit(solution)/shard_map/mul | solution.py:42
  105.8 3.9 %select_convert_fusion.1 = (bf16[1,3,256,1024]{3,2,1,0:T(8,128)(2,1)S(1)}, f32[1,3,256,1024]{3,2,1,0:T(8,128)S(1)}) fusion(pred[1,3,256,1024]{3,2,1,0:T(8,128)(4,1)S(1)} %broadcast_in_dim.46, f32[1024]{0:T(1024)S(1)} %get-tuple-element.20, f32[1,3,256,1024]{3,2,1,0:T(8,128)} %mul.334, f32[1,3,256,1024]{3,2,1,0:T(8,128)} %mul.341, ...), kind=kLoop, calls=%fused_computation.7 | loop fusion | flops 12582912 | bytes 11812864 | tf_op jit(solution)/shard_map/convert_element_type | solution.py:240
  111.1 2.4 pad_maximum_fusion.band_ref
  114.7 26.9 %all-to-all-done.1 = bf16[16,2,272,128]{3,2,1,0:T(8,128)(2,1)} async-done(((bf16[16,2,272,128]{3,2,1,0:T(8,128)(2,1)}), bf16[16,2,272,128]{3,2,1,0:T(8,128)(2,1)}, u32[]{:S(2)}, u32[]{:S(2)}) %all-to-all-start.1) | async-done | bytes 2228256 | tf_op jit(solution)/shard_map/all_to_all | solution.py:275
  141.6 1.9 copy_bitcast_fusion.1
  145.6 4.0 %collective-permute-start.1 = (bf16[2,272,8]{2,1,0:T(8,128)(2,1)}, bf16[2,272,8]{2,1,0:T(8,128)(2,1)S(1)}, u32[]{:S(2)}, u32[]{:S(2)}) collective-permute-start(bf16[2,272,8]{2,1,0:T(8,128)(2,1)} %get-tuple-element.10), channel_id=1, source_target_pairs={{16,0},{17,1},{18,2},{19,3},{20,4},{21,5},{22,6},{23,7},{24,8},{25... | collective-permute-start | bytes 26120 | tf_op jit(solution)/shard_map/ppermute | solution.py:280
  150.8 3.2 %gather_fusion = f32[72,128,128]{1,2,0:T(8,128)} fusion(f32[16,128,128]{1,2,0:T(8,128)S(1)} %bitcast.79, s32[1024]{0:T(1024)} %pad_clamp_fusion), kind=kCustom, calls=%fused_computation | custom fusion | bytes 9437472 | tf_op jit(solution)/shard_map/jit(_take)/gather | solution.py:295
  154.0 5.7 %copy.27 = f32[4,18,128,128]{2,0,3,1:T(4,128)S(1)} copy(f32[4,18,128,128]{2,3,1,0:T(8,128)} %bitcast.81) | data formatting | bytes 9437184 | tf_op jit(solution)/shard_map/jit(_take)/gather | solution.py:295
  160.2 2.7 %slice.33 = f32[272,2176]{0,1:T(8,128)} slice(f32[512,2304]{0,1:T(8,128)S(1)} %bitcast.83), slice={[120:392], [120:2296]} | slice | bytes 4734976 | tf_op jit(solution)/shard_map/slice | solution.py:298
  162.8 3.6 %copy.31 = f32[272,2176]{1,0:T(8,128)} copy(f32[272,2176]{0,1:T(8,128)} %slice.33) | data formatting | bytes 4734976
  166.4 4.0 %concatenate.3 = bf16[2,272,2176]{2,1,0:T(8,128)(2,1)} concatenate(bf16[2,272,8]{2,1,0:T(8,128)(2,1)S(1)} %collective-permute-done, bf16[2,272,2048]{2,1,0:T(8,128)(2,1)S(1)} %copy_bitcast_fusion.1, bf16[2,272,8]{2,1,0:T(8,128)(2,1)S(1)} %collective-permute-done.1, bf16[2,272,112]{2,1,0:T(8,128)(2,1)S(1)} %broadcast_in_dim.42), dimensions={2} | concatenate | bytes 4734976 | tf_op jit(solution)/shard_map/concatenate | solution.py:283
  170.4 2.1 convert_element_type.83
  172.8 1.9 fusion.10
  175.6 75.7 %shard_map.129 = f32[256,2048]{1,0:T(8,128)S(1)} custom-call(bf16[3,272,2176]{2,1,0:T(8,128)(2,1)S(1)} %fusion.term_ref, bf16[3,3,256,1024]{3,2,1,0:T(8,128)(2,1)} %pad_maximum_fusion.band_ref), custom_call_target="tpu_custom_call" | custom-call | tf_op jit(solution)/shard_map/pallas_call | solution.py:202
  (75 shorter events, 20.6 us)
Async XLA Ops:
  0.0 150.8 %copy-start = (f32[16,128,128]{2,1,0:T(8,128)S(1)}, f32[16,128,128]{2,1,0:T(8,128)}, u32[]{:S(2)}) copy-start(f32[16,128,128]{2,1,0:T(8,128)} %param.14) | copy-start | bytes 3145732
  1.5 2.8 %copy-start.2 = (bf16[256,256]{1,0:T(8,128)(2,1)S(1)}, bf16[256,256]{1,0:T(8,128)(2,1)}, u32[]{:S(2)}) copy-start(bf16[256,256]{1,0:T(8,128)(2,1)} %constant.89.clone.big_ref) | copy-start | bytes 393220
  1.5 2.8 %copy-start.3 = (bf16[256,256]{1,0:T(8,128)(2,1)S(1)}, bf16[256,256]{1,0:T(8,128)(2,1)}, u32[]{:S(2)}) copy-start(bf16[256,256]{1,0:T(8,128)(2,1)} %constant.90.clone.small_ref) | copy-start | bytes 393220
  1.5 2.8 %copy-start.4 = (f32[32,128]{1,0:T(8,128)S(1)}, f32[32,128]{1,0:T(8,128)}, u32[]{:S(2)}) copy-start(f32[32,128]{1,0:T(8,128)} %constant.87.clone.cos_ref) | copy-start | bytes 49156
  1.5 2.8 %copy-start.5 = (f32[32,128]{1,0:T(8,128)S(1)}, f32[32,128]{1,0:T(8,128)}, u32[]{:S(2)}) copy-start(f32[32,128]{1,0:T(8,128)} %constant.88.clone.sin_ref) | copy-start | bytes 49156
  12.9 6.3 %copy-start.13 = (s32[4]{0:T(128)S(1)}, s32[4]{0:T(128)}, u32[]{:S(2)}) copy-start(s32[4]{0:T(128)} %param.17) | copy-start | bytes 52
  12.9 6.3 %copy-start.14 = (s32[4]{0:T(128)S(1)}, s32[4]{0:T(128)}, u32[]{:S(2)}) copy-start(s32[4]{0:T(128)} %param.16) | copy-start | bytes 52
  12.9 18.2 %copy-start.12 = (s32[16,4]{0,1:T(4,128)S(1)}, s32[16,4]{0,1:T(4,128)}, u32[]{:S(2)}) copy-start(s32[16,4]{0,1:T(4,128)} %param.15) | copy-start | bytes 772
  12.9 60.1 %all-to-all-start = ((bf16[32,2,128,128]{3,2,1,0:T(8,128)(2,1)}), bf16[32,2,128,128]{3,2,1,0:T(8,128)(2,1)S(1)}, u32[]{:S(2)}, u32[]{:S(2)}) async-start(bf16[32,2,128,128]{3,2,1,0:T(8,128)(2,1)} %shard_map.127), calls=%async_computation | async-start | bytes 4194304 | tf_op jit(solution)/shard_map/all_to_all | solution.py:269
  82.0 9.1 %copy-start.10 = (s32[2,4,2]{1,2,0:T(2,128)S(1)}, s32[2,4,2]{1,2,0:T(2,128)}, u32[]{:S(2)}) copy-start(s32[2,4,2]{1,2,0:T(2,128)} %all-gather.2) | copy-start | bytes 196
  82.0 10.4 %copy-start.8 = (f32[768,128]{1,0:T(8,128)S(1)}, f32[768,128]{1,0:T(8,128)}, u32[]{:S(2)}) copy-start(f32[768,128]{1,0:T(8,128)} %subtract_convert_fusion) | copy-start | bytes 1179652
  82.0 59.6 %all-to-all-start.1 = ((bf16[16,2,272,128]{3,2,1,0:T(8,128)(2,1)}), bf16[16,2,272,128]{3,2,1,0:T(8,128)(2,1)}, u32[]{:S(2)}, u32[]{:S(2)}) async-start(bf16[16,2,272,128]{3,2,1,0:T(8,128)(2,1)} %shard_map.128), calls=%async_computation.1 | async-start | bytes 4456448 | tf_op jit(solution)/shard_map/all_to_all | solution.py:275
  94.3 4.6 %copy-start.9 = (s32[768]{0:T(1024)S(1)}, s32[768]{0:T(1024)}, u32[]{:S(2)}) copy-start(s32[768]{0:T(1024)} %sub.128) | copy-start | bytes 9220
  94.3 4.6 %copy-start.11 = (s32[128]{0:T(128)S(1)}, s32[128]{0:T(128)}, u32[]{:S(2)}) copy-start(s32[128]{0:T(128)} %iota.184) | copy-start | bytes 1540
  144.3 22.1 %collective-permute-start = (bf16[2,272,8]{2,1,0:T(8,128)(2,1)}, bf16[2,272,8]{2,1,0:T(8,128)(2,1)S(1)}, u32[]{:S(2)}, u32[]{:S(2)}) collective-permute-start(bf16[2,272,8]{2,1,0:T(8,128)(2,1)} %get-tuple-element.11), channel_id=1, source_target_pairs={{0,16},{1,17},{2,18},{3,19},{4,20},{5,21},{6,22},{7,23},{8,24},{9,... | collective-permute-start | bytes 26120 | tf_op jit(solution)/shard_map/ppermute | solution.py:279
  145.6 20.8 %collective-permute-start.1 = (bf16[2,272,8]{2,1,0:T(8,128)(2,1)}, bf16[2,272,8]{2,1,0:T(8,128)(2,1)S(1)}, u32[]{:S(2)}, u32[]{:S(2)}) collective-permute-start(bf16[2,272,8]{2,1,0:T(8,128)(2,1)} %get-tuple-element.10), channel_id=1, source_target_pairs={{16,0},{17,1},{18,2},{19,3},{20,4},{21,5},{22,6},{23,7},{24,8},{25... | collective-permute-start | bytes 26120 | tf_op jit(solution)/shard_map/ppermute | solution.py:280
  170.4 2.4 copy-start.6
  172.8 1.9 copy-start.7
  175.6 77.5 %copy-start.1 = (f32[16,128,128]{2,1,0:T(8,128)S(1)}, f32[16,128,128]{2,1,0:T(8,128)}, u32[]{:S(2)}) copy-start(f32[16,128,128]{2,1,0:T(8,128)} %param.14) | copy-start | bytes 3145732

commit v2 on v1

--- a/solution.py
+++ b/solution.py
@@ -17,6 +17,7 @@
 TILE_LANES = 16
 GROUPS = LANES // TILE_LANES
 PHASE = TILE_ROWS * TILE_LANES
+STEP_TILES = 8
 
 nugget_share = 0.3
 peak_share = 1024.0 / (2.0 * math.pi)
@@ -144,14 +145,10 @@
 def swap_groups(cells):
     row = lax.broadcasted_iota(jnp.int32, cells.shape, 1)
     group = lax.broadcasted_iota(jnp.int32, cells.shape, 2) // TILE_LANES
-    for bit in (4, 2, 1):
-        row_set = (row & bit) != 0
-        group_set = (group & bit) != 0
-        lane = bit * TILE_LANES
-        down = pltpu.roll(pltpu.roll(cells, TILE_ROWS - bit, 1), lane, 2)
-        up = down if bit == 4 else pltpu.roll(pltpu.roll(cells, bit, 1), LANES - lane, 2)
-        cells = jnp.where(row_set == group_set, cells, jnp.where(group_set, down, up))
-    return cells
+    skewed = pltpu.roll(cells, 0, 2, stride=TILE_LANES, stride_axis=1)
+    picked = jnp.take_along_axis(skewed, (group + row - 7) & 7, axis=1)
+    level = pltpu.roll(picked, TILE_LANES, 2, stride=TILE_LANES, stride_axis=1)
+    return jnp.take_along_axis(level, 7 - row, axis=1)
 
 
 def stability_kernel(families, term_ref, band_ref, out_ref, swapped, gathered):
@@ -173,24 +170,27 @@
                 gathered[term, both, :, 0:PHASE] = swapped[:, 0:across, :].astype(jnp.bfloat16)
                 gathered[term, both, :, PHASE:] = swapped[:, 1 : across + 1, :].astype(jnp.bfloat16)
 
-    tile = pl.program_id(0) * 2
+    tile = pl.program_id(0) * STEP_TILES
     low = None
     for pair in range(families // 2):
         lanes = slice(pair * 2 * PHASE, (pair + 1) * 2 * PHASE)
-        resisting = driving = None
-        for shift in range(3):
-            for term in range(3):
-                left = gathered[term, pl.ds(tile + shift, 2)].reshape(2 * across, 2 * PHASE)
-                got = jnp.dot(left, band_ref[term, shift, :, lanes], preferred_element_type=jnp.float32)
-                if term == 2:
-                    driving = got if driving is None else driving + got
-                else:
-                    resisting = got if resisting is None else resisting + got
-        ratio = resisting / driving
+
+        def total(chosen):
+            pieces = [(term, shift) for term in chosen for shift in range(3)]
+            left = [gathered[term, pl.ds(tile + shift, STEP_TILES)] for term, shift in pieces]
+            left = [piece.reshape(STEP_TILES * across, 2 * PHASE) for piece in left]
+            right = [band_ref[term, shift, :, lanes] for term, shift in pieces]
+            return jnp.dot(
+                jnp.concatenate(left, axis=1),
+                jnp.concatenate(right, axis=0),
+                preferred_element_type=jnp.float32,
+            )
+
+        ratio = total((0, 1)) / total((2,))
         least = jnp.minimum(ratio[:, 0:PHASE], ratio[:, PHASE:])
         low = least if low is None else jnp.minimum(low, least)
-    turned = swap_groups(low.reshape(2 * chunks, TILE_ROWS, LANES))
-    for side in range(2):
+    turned = swap_groups(low.reshape(STEP_TILES * chunks, TILE_ROWS, LANES))
+    for side in range(STEP_TILES):
         for chunk in range(chunks):
             out_ref[side * 8 : side * 8 + 8, chunk * LANES : (chunk + 1) * LANES] = turned[side * chunks + chunk]
 
@@ -201,18 +201,18 @@
     tiles = height // TILE_ROWS + 2
     return pl.pallas_call(
         functools.partial(stability_kernel, families),
-        grid=(height // 16,),
+        grid=(height // (TILE_ROWS * STEP_TILES),),
         out_shape=jax.ShapeDtypeStruct((height, width), jnp.float32),
         in_specs=[
             pl.BlockSpec(terms.shape, lambda i: (0, 0, 0), pipeline_mode=pl.Buffered(1)),
             pl.BlockSpec(band.shape, lambda i: (0, 0, 0, 0), pipeline_mode=pl.Buffered(1)),
         ],
-        out_specs=pl.BlockSpec((16, width), lambda i: (i, 0)),
+        out_specs=pl.BlockSpec((TILE_ROWS * STEP_TILES, width), lambda i: (i, 0)),
         scratch_shapes=[
             pltpu.VMEM((2, across + GROUPS, LANES), jnp.float32),
             pltpu.VMEM((3, tiles, across, 2 * PHASE), jnp.bfloat16),
         ],
-        compiler_params=pltpu.CompilerParams(vmem_limit_bytes=48 << 20),
+        compiler_params=pltpu.CompilerParams(vmem_limit_bytes=56 << 20),
     )(terms, band)
 
 
@@ -254,11 +254,18 @@
     window_rows = side_cells // row_count
     window_columns = side_cells // (col_count * split)
 
-    families = lax.all_gather(
-        jnp.stack([family_heading_index, family_extent_index]), "orient", axis=1, tiled=True
+    tiles_down, tiles_over = tile_choice_index.shape
+    told = jnp.concatenate(
+        [tile_choice_index.reshape(-1), family_heading_index, family_extent_index]
     )
-    choices = lax.all_gather(tile_choice_index, "row", axis=0, tiled=True)
-    choices = lax.all_gather(choices, "col", axis=1, tiled=True)
+    told = lax.all_gather(told, ("row", "col", "orient"))
+    told = told.reshape(row_count, col_count, split, told.shape[1])
+    noise, told = lax.optimization_barrier((noise, told))
+    area = tiles_down * tiles_over
+    choices = told[:, :, 0, :area].reshape(row_count, col_count, tiles_down, tiles_over)
+    choices = choices.transpose(0, 2, 1, 3).reshape(row_count * tiles_down, col_count * tiles_over)
+    families = told[0, 0, :, area:].reshape(split, 2, -1)
+    families = families.transpose(1, 0, 2).reshape(2, -1)
 
     own = lax.dynamic_slice_in_dim(noise, side * lines, lines, 1)
     first_line = lax.axis_index(("row", "col", "orient")) * lines
@@ -267,23 +274,9 @@
     weights = own * amplitude(u_index, v_index, side_cells)[None]
     spectrum = transform(weights, False, lines, side_cells, devices, 0)
     held = lax.all_to_all(spectrum, ("row", "col", "orient"), split_axis=0, concat_axis=0, tiled=True)
-    positions = side_cells // devices
-    per_block = LANES // lines
-    held = held.reshape(side_cells // LANES, per_block, 2, positions, lines)
-    held = held.transpose(0, 2, 3, 1, 4).reshape(side_cells // LANES, 2, positions, LANES)
-    fields = transform(held, True, positions, side_cells, col_count * split, R)
-    fields = lax.all_to_all(fields, ("col", "orient"), split_axis=0, concat_axis=0, tiled=True)
     tall = window_columns + 2 * R
-    fields = fields.transpose(1, 2, 0, 3).reshape(2, tall, window_rows)
-    ends = row_count - 1
-    before = lax.ppermute(fields[:, :, window_rows - R :], "row", [(i, i + 1) for i in range(ends)])
-    after = lax.ppermute(fields[:, :, :R], "row", [(i + 1, i) for i in range(ends)])
     wide = (window_rows // LANES + 1) * LANES
     spare = wide - window_rows - 2 * R
-    fields = jnp.concatenate(
-        [before, fields, after, jnp.zeros((2, tall, spare), fields.dtype)], axis=2
-    ).astype(jnp.float32)
-
     tile_side = elevation_library.shape[1]
     tiles_x = window_rows // tile_side
     tiles_y = window_columns // tile_side
@@ -300,11 +293,28 @@
     x = row * window_rows - R + lax.broadcasted_iota(jnp.int32, (tall, wide), 1)
     inside = (y >= 0) & (y < side_cells) & (x >= 0) & (x < side_cells)
     secant = jnp.sqrt(1.0 + slope * slope)
-    cohesion = 0.5 * jnp.exp(0.4 * fields[0])
-    friction = 0.6 * jnp.exp(0.25 * fields[1])
-    terms = jnp.stack([cohesion * secant, friction / secant, slope / secant])
-    terms = jnp.where(inside[None], terms, 0.0).astype(jnp.bfloat16)
+    lift = jnp.where(inside, 0.5 * secant, 0.0)
+    grip = jnp.where(inside, 0.6 / secant, 0.0)
+    drive = jnp.where(inside, slope / secant, 0.0).astype(jnp.bfloat16)
     band = band_weights(families[0], families[1])
+    held, lift, grip, drive, band = lax.optimization_barrier((held, lift, grip, drive, band))
+    positions = side_cells // devices
+    per_block = LANES // lines
+    held = held.reshape(side_cells // LANES, per_block, 2, positions, lines)
+    held = held.transpose(0, 2, 3, 1, 4).reshape(side_cells // LANES, 2, positions, LANES)
+    fields = transform(held, True, positions, side_cells, col_count * split, R)
+    fields = lax.all_to_all(fields, ("col", "orient"), split_axis=0, concat_axis=0, tiled=True)
+    fields = fields.transpose(1, 2, 0, 3).reshape(2, tall, window_rows)
+    ends = row_count - 1
+    before = lax.ppermute(fields[:, :, window_rows - R :], "row", [(i, i + 1) for i in range(ends)])
+    after = lax.ppermute(fields[:, :, :R], "row", [(i + 1, i) for i in range(ends)])
+    fields = jnp.concatenate(
+        [before, fields, after, jnp.zeros((2, tall, spare), fields.dtype)], axis=2
+    ).astype(jnp.float32)
+
+    cohesion = (jnp.exp(0.4 * fields[0]) * lift).astype(jnp.bfloat16)
+    friction = (jnp.exp(0.25 * fields[1]) * grip).astype(jnp.bfloat16)
+    terms = jnp.stack([cohesion, friction, drive])
     return stability(terms, band, window_columns, window_rows).T
 
 

time: 254 us -> 244 us (0.961)
  blocking collectives: 48.4 us -> 96.7 us
  Pallas kernels: 93.3 us -> 47.6 us
  waiting for transfers between devices: 26.9 us -> 5.14 us
  local copies, waits for them, and re-layouts: 42.1 us -> 55.5 us
  starting transfers between devices: 19.9 us -> 9.4 us
  other arithmetic: 22.2 us -> 26.2 us
    all_to_all x0 -> x1, blocking collectives: none -> 57.1 us  [body(): lax.all_to_all(fields, ('col', 'orient'), split_axis=0, concat_axis=0, ti...]
    all_gather x3 -> x0, blocking collectives: 48.4 us -> none  [the longest x1 32.8 us: body(): choices = lax.all_gather(choices, 'col', axis=1, tiled=True)]
    pallas_call x1, Pallas kernels: 75.7 us -> 31.5 us  [stability(): pl.pallas_call(functools.partial(stability_kernel, families), grid=(heigh...]
    unnamed x0 -> x1, blocking collectives: none -> 39.6 us
    all_to_all x1 -> x0, waiting for transfers between devices: 26.9 us -> none  [body(): lax.all_to_all(fields, ('col', 'orient'), split_axis=0, concat_axis=0, ti...]
    all_to_all x1 -> x0, starting transfers between devices: 8.37 us -> none  [body(): lax.all_to_all(fields, ('col', 'orient'), split_axis=0, concat_axis=0, ti...]
    ppermute x1, waiting for transfers between devices: 0.01 us -> 3.8 us  [body(): lax.ppermute(fields[:, :, window_rows - R:], 'row', [(i, i + 1) for i in...]
    convert_element_type x1, other arithmetic: 0.83 us -> 4.22 us  [body(): drive = jnp.where(inside, slope / secant, 0.0).astype(jnp.bfloat16)]
  transfers between devices with their start and end apart: 4 -> 3, of which waited for: 1 -> 2; matrix products, arithmetic and copies ran while one was open for 18% -> 25% of each run, Pallas kernels for 0% -> 0%
where the time goes in v2:
time: 244 us; the launch traced here: 241 us
  blocking collectives  96.7 us (40%)
  local copies, waits for them, and re-layouts  55.5 us (23%)
  Pallas kernels  47.6 us (20%)
  other arithmetic  26.2 us (11%)
  starting transfers between devices  9.4 us (4%)
  waiting for transfers between devices  5.14 us (2%)
    all_to_all x1, blocking collectives, body(): lax.all_to_all(fields, ('col', 'orient'), split_axis=0, concat_axis=0, ti...  57.1 us
    unnamed x1, blocking collectives  39.6 us
    pallas_call x1, Pallas kernels, stability(): pl.pallas_call(functools.partial(stability_kernel, families), grid=(heigh...  31.5 us
    pallas_call x2, Pallas kernels, transform(): pl.pallas_call(functools.partial(transform_kernel, planes, blocks, span,...  16.1 us
    mul x5, local copies, waits for them, and re-layouts, ellipsoid(): along = offset_u * jnp.cos(heading) + offset_v * jnp.sin(heading)  14.9 us
    gather x2, local copies, waits for them, and re-layouts, body(): jnp.take(elevation_library.transpose(0, 2, 1), local.T, axis=0, mode='clip')  8.66 us
    unnamed x34, local copies, waits for them, and re-layouts  7 us
    all_to_all x1, starting transfers between devices, body(): lax.all_to_all(spectrum, ('row', 'col', 'orient'), split_axis=0, concat_a...  5.95 us
  transfers between devices with their start and end apart: 3, of which 2 were waited for; matrix products, arithmetic and copies ran while one was open for 25% of the time, Pallas kernels for 0%

profile of v2, /device:TPU:13, one launch (start us, length us, event | category | flops | bytes accessed | tf_op | source)
XLA Modules:
  0.0 240.8 jit_solution(1806138054584998815)
XLA Ops:
  1.9 39.6 %all-reduce.1 = s32[2304]{0:T(1024)S(1)} all-reduce(s32[2304]{0:T(1024)S(1)} %add_dynamic-update-slice_fusion), channel_id=2, replica_groups=mesh['row'=2,'col'=8,'orient'=2] {'row','col','orient'}, use_global_device_ids=true, to_apply=%add.1 | all-reduce | flops 2304 | bytes 18432
  43.0 2.8 %dynamic-slice_multiply_fusion.in_ref = f32[2,128,4096]{2,1,0:T(8,128)S(1)} fusion(f32[2,256,4096]{2,1,0:T(8,128)} %param.13, s32[]{:T(128)S(6)} %select_n.40, f32[128,4096]{1,0:T(8,128)S(1)} %fusion.11), kind=kLoop, calls=%fused_computation.3 | loop fusion | flops 1048576 | bytes 10485764 | tf_op jit(solution)/shard_map/mul | solution.py:274
  45.9 8.5 %shard_map.127 = bf16[32,2,128,128]{3,2,1,0:T(8,128)(2,1)} custom-call(f32[2,128,4096]{2,1,0:T(8,128)S(1)} %dynamic-slice_multiply_fusion.in_ref, f32[32,128]{1,0:T(8,128)S(1)} %copy-done.5, f32[32,128]{1,0:T(8,128)S(1)} %copy-done.4, bf16[256,256]{1,0:T(8,128)(2,1)S(1)} %copy-done.3, bf16[256,256]{1,0:T(8,128)(2,1)S(1)} %copy-done.2), custom_call_target="tpu_custom_call" | custom-call | tf_op jit(solution)/shard_map/pallas_call | solution.py:132
  54.4 6.0 %all-to-all-start = ((bf16[32,2,128,128]{3,2,1,0:T(8,128)(2,1)}), bf16[32,2,128,128]{3,2,1,0:T(8,128)(2,1)S(1)}, u32[]{:S(2)}, u32[]{:S(2)}) async-start(bf16[32,2,128,128]{3,2,1,0:T(8,128)(2,1)} %shard_map.127), calls=%async_computation | async-start | bytes 4194304 | tf_op jit(solution)/shard_map/all_to_all | solution.py:276
  75.9 3.3 %broadcast_in_dim.37 = pred[1,3,256,1024]{3,2,1,0:T(8,128)(4,1)} reshape(pred[768,8,128]{2,1,0:T(8,128)(4,1)} %broadcast_in_dim.36) | data formatting | bytes 1572864 | tf_op jit(solution)/shard_map/jit(_where)/broadcast_in_dim | solution.py:240
  79.1 2.8 %mul.315 = f32[768,8,128]{2,1,0:T(8,128)} broadcast(f32[768,128]{1,0:T(8,128)} %subtract_convert_fusion), dimensions={0,2} | broadcast | bytes 3538944 | tf_op jit(solution)/shard_map/mul | solution.py:43
  81.9 4.5 %mul.316 = f32[1,3,256,1024]{3,2,1,0:T(8,128)} reshape(f32[768,8,128]{2,1,0:T(8,128)} %mul.315) | data formatting | bytes 6291456 | tf_op jit(solution)/shard_map/mul | solution.py:43
  86.5 3.0 %mul.322 = f32[768,8,128]{2,1,0:T(8,128)} broadcast(f32[768,128]{1,0:T(8,128)} %subtract_convert_fusion.1), dimensions={0,2} | broadcast | bytes 3538944 | tf_op jit(solution)/shard_map/mul | solution.py:43
  89.4 4.5 %mul.323 = f32[1,3,256,1024]{3,2,1,0:T(8,128)} reshape(f32[768,8,128]{2,1,0:T(8,128)} %mul.322) | data formatting | bytes 6291456 | tf_op jit(solution)/shard_map/mul | solution.py:43
  94.0 3.0 %gather_fusion = f32[72,128,128]{1,2,0:T(8,128)} fusion(f32[16,128,128]{1,2,0:T(8,128)S(1)} %bitcast.60, s32[1024]{0:T(1024)S(1)} %pad_clamp_fusion), kind=kCustom, calls=%fused_computation | custom fusion | bytes 9437472 | tf_op jit(solution)/shard_map/jit(_take)/gather | solution.py:288
  97.0 5.7 %copy.28 = f32[4,18,128,128]{2,0,3,1:T(4,128)S(1)} copy(f32[4,18,128,128]{2,3,1,0:T(8,128)} %bitcast.61) | data formatting | bytes 9437184 | tf_op jit(solution)/shard_map/jit(_take)/gather | solution.py:288
  103.2 2.8 %slice.40 = f32[272,2176]{0,1:T(8,128)} slice(f32[512,2304]{0,1:T(8,128)S(1)} %bitcast.63), slice={[120:392], [120:2296]} | slice | bytes 4734976 | tf_op jit(solution)/shard_map/slice | solution.py:291
  105.9 3.7 %copy.32 = f32[272,2176]{1,0:T(8,128)} copy(f32[272,2176]{0,1:T(8,128)} %slice.40) | data formatting | bytes 4734976
  109.9 3.9 %select_convert_fusion.1 = (bf16[1,3,256,1024]{3,2,1,0:T(8,128)(2,1)S(1)}, f32[1,3,256,1024]{3,2,1,0:T(8,128)S(1)}) fusion(pred[1,3,256,1024]{3,2,1,0:T(8,128)(4,1)S(1)} %copy-done.9, f32[1024]{0:T(1024)S(1)} %get-tuple-element.36, f32[1,3,256,1024]{3,2,1,0:T(8,128)} %mul.316, f32[1,3,256,1024]{3,2,1,0:T(8,128)} %mul.323, f32[1024]{0:T(1024)S(1)} %get-tuple-element.37, ...), kind=kLoop, calls=%fused_computation.6 | loop fusion | flops 12582912 | bytes 11812864 | tf_op jit(solution)/shard_map/convert_element_type | solution.py:240
  115.3 2.4 pad_maximum_fusion.band_ref
  117.9 4.2 %select_convert_fusion.2 = (bf16[272,2176]{1,0:T(8,128)(2,1)}, f32[272,2176]{1,0:T(8,128)}, f32[272,2176]{1,0:T(8,128)}) fusion(f32[272,2176]{1,0:T(8,128)S(1)} %copy-done.8, pred[2176]{0:T(1024)(128)(4,1)S(1)} %get-tuple-element.33, pred[2176]{0:T(1024)(128)(4,1)S(1)} %get-tuple-element.34, pred[272]{0:T(512)(128)(4,1)S(1)} %fusion.26), kind=kLoop, calls=%fused_computation.19 | loop fusion | flops 6510592 | bytes 8290832 | tf_op jit(solution)/shard_map/convert_element_type | solution.py:298
  122.2 7.6 %shard_map.128 = bf16[16,2,272,128]{3,2,1,0:T(8,128)(2,1)S(1)} custom-call(bf16[32,2,128,128]{3,2,1,0:T(8,128)(2,1)S(1)} %all-to-all-done.in_ref, f32[32,128]{1,0:T(8,128)S(1)} %copy-done.5, f32[32,128]{1,0:T(8,128)S(1)} %copy-done.4, bf16[256,256]{1,0:T(8,128)(2,1)S(1)} %copy-done.3, bf16[256,256]{1,0:T(8,128)(2,1)S(1)} %copy-done.2), custom_call_target="tpu_custom_call" | custom-call | tf_op jit(solution)/shard_map/pallas_call | solution.py:132
  129.8 57.1 %all_to_all.10 = bf16[16,2,272,128]{3,2,1,0:T(8,128)(2,1)S(1)} all-to-all(bf16[16,2,272,128]{3,2,1,0:T(8,128)(2,1)S(1)} %shard_map.128), channel_id=1, replica_groups=mesh['row'=2,'col'=8,'orient'=2] {'col','orient'}, dimensions={0} | all-to-all | bytes 4456448 | tf_op jit(solution)/shard_map/all_to_all | solution.py:306
  187.3 2.2 collective-permute-start.1
  192.1 3.8 %collective-permute-done = bf16[2,272,8]{2,1,0:T(8,128)(2,1)S(1)} collective-permute-done((bf16[2,272,8]{2,1,0:T(8,128)(2,1)S(1)}, bf16[2,272,8]{2,1,0:T(8,128)(2,1)S(1)}, u32[]{:S(2)}, u32[]{:S(2)}) %collective-permute-start) | collective-permute-done | bytes 8736 | tf_op jit(solution)/shard_map/ppermute | solution.py:309
  195.9 4.2 %concatenate.7 = bf16[2,272,2176]{2,1,0:T(8,128)(2,1)} concatenate(bf16[2,272,8]{2,1,0:T(8,128)(2,1)S(1)} %collective-permute-done, bf16[2,272,2048]{2,1,0:T(8,128)(2,1)S(1)} %copy_bitcast_fusion.1, bf16[2,272,8]{2,1,0:T(8,128)(2,1)S(1)} %collective-permute-done.1, bf16[2,272,112]{2,1,0:T(8,128)(2,1)S(1)} %broadcast_in_dim.38), dimensions={2} | concatenate | bytes 4734976 | tf_op jit(solution)/shard_map/concatenate | solution.py:311
  200.1 2.1 convert_element_type.96
  206.5 31.5 %shard_map.129 = f32[256,2048]{1,0:T(8,128)} custom-call(bf16[3,272,2176]{2,1,0:T(8,128)(2,1)} %pad_maximum_fusion.1.term_ref, bf16[3,3,256,1024]{3,2,1,0:T(8,128)(2,1)} %pad_maximum_fusion.band_ref), custom_call_target="tpu_custom_call" | custom-call | tf_op jit(solution)/shard_map/pallas_call | solution.py:202
  237.9 2.9 %copy.31 = f32[2048,256]{1,0:T(8,128)} copy(f32[2048,256]{0,1:T(8,128)} %bitcast.64) | data formatting | bytes 4194304 | tf_op jit(solution)/shard_map/transpose | solution.py:318
  (81 shorter events, 28.5 us)
Async XLA Ops:
  0.0 94.0 %copy-start = (f32[16,128,128]{2,1,0:T(8,128)S(1)}, f32[16,128,128]{2,1,0:T(8,128)}, u32[]{:S(2)}) copy-start(f32[16,128,128]{2,1,0:T(8,128)} %param.14) | copy-start | bytes 3145732
  43.0 2.9 %copy-start.2 = (bf16[256,256]{1,0:T(8,128)(2,1)S(1)}, bf16[256,256]{1,0:T(8,128)(2,1)}, u32[]{:S(2)}) copy-start(bf16[256,256]{1,0:T(8,128)(2,1)} %constant.90.clone.small_ref) | copy-start | bytes 393220
  43.0 2.9 %copy-start.3 = (bf16[256,256]{1,0:T(8,128)(2,1)S(1)}, bf16[256,256]{1,0:T(8,128)(2,1)}, u32[]{:S(2)}) copy-start(bf16[256,256]{1,0:T(8,128)(2,1)} %constant.89.clone.big_ref) | copy-start | bytes 393220
  43.0 2.9 %copy-start.4 = (f32[32,128]{1,0:T(8,128)S(1)}, f32[32,128]{1,0:T(8,128)}, u32[]{:S(2)}) copy-start(f32[32,128]{1,0:T(8,128)} %constant.88.clone.sin_ref) | copy-start | bytes 49156
  43.0 2.9 %copy-start.5 = (f32[32,128]{1,0:T(8,128)S(1)}, f32[32,128]{1,0:T(8,128)}, u32[]{:S(2)}) copy-start(f32[32,128]{1,0:T(8,128)} %constant.87.clone.cos_ref) | copy-start | bytes 49156
  54.4 67.7 %all-to-all-start = ((bf16[32,2,128,128]{3,2,1,0:T(8,128)(2,1)}), bf16[32,2,128,128]{3,2,1,0:T(8,128)(2,1)S(1)}, u32[]{:S(2)}, u32[]{:S(2)}) async-start(bf16[32,2,128,128]{3,2,1,0:T(8,128)(2,1)} %shard_map.127), calls=%async_computation | async-start | bytes 4194304 | tf_op jit(solution)/shard_map/all_to_all | solution.py:276
  61.8 0.5 copy-start.11
  105.9 3.7 %copy-start.12 = (f32[8]{0:T(128)S(1)}, f32[8]{0:T(128)}, u32[]{:S(2)}) copy-start(f32[8]{0:T(128)} %add.165) | copy-start | bytes 100
  105.9 3.8 %copy-start.13 = (f32[8]{0:T(128)S(1)}, f32[8]{0:T(128)}, u32[]{:S(2)}) copy-start(f32[8]{0:T(128)} %cos.13) | copy-start | bytes 100
  105.9 3.8 %copy-start.14 = (f32[8]{0:T(128)S(1)}, f32[8]{0:T(128)}, u32[]{:S(2)}) copy-start(f32[8]{0:T(128)} %sin.13) | copy-start | bytes 100
  105.9 4.0 %copy-start.9 = (pred[1,3,256,1024]{3,2,1,0:T(8,128)(4,1)S(1)}, pred[1,3,256,1024]{3,2,1,0:T(8,128)(4,1)}, u32[]{:S(2)}) copy-start(pred[1,3,256,1024]{3,2,1,0:T(8,128)(4,1)} %broadcast_in_dim.37) | copy-start | bytes 2359300
  115.2 2.7 %copy-start.8 = (f32[272,2176]{1,0:T(8,128)S(1)}, f32[272,2176]{1,0:T(8,128)}, u32[]{:S(2)}) copy-start(f32[272,2176]{1,0:T(8,128)} %copy.32) | copy-start | bytes 7102468
  187.3 4.8 %collective-permute-start.1 = (bf16[2,272,8]{2,1,0:T(8,128)(2,1)S(1)}, bf16[2,272,8]{2,1,0:T(8,128)(2,1)S(1)}, u32[]{:S(2)}, u32[]{:S(2)}) collective-permute-start(bf16[2,272,8]{2,1,0:T(8,128)(2,1)S(1)} %get-tuple-element.29), channel_id=1, source_target_pairs={{16,0},{17,1},{18,2},{19,3},{20,4},{21,5},{22,6},{23,7},{24,8},{25... | collective-permute-start | bytes 26120 | tf_op jit(solution)/shard_map/ppermute | solution.py:310
  189.5 6.4 %collective-permute-start = (bf16[2,272,8]{2,1,0:T(8,128)(2,1)S(1)}, bf16[2,272,8]{2,1,0:T(8,128)(2,1)S(1)}, u32[]{:S(2)}, u32[]{:S(2)}) collective-permute-start(bf16[2,272,8]{2,1,0:T(8,128)(2,1)S(1)} %get-tuple-element.30), channel_id=1, source_target_pairs={{0,16},{1,17},{2,18},{3,19},{4,20},{5,21},{6,22},{7,23},{8,24},{9,... | collective-permute-start | bytes 26120 | tf_op jit(solution)/shard_map/ppermute | solution.py:309
  200.1 2.4 copy-start.6
  200.1 3.1 %copy-start.7 = (f32[272,2176]{1,0:T(8,128)S(1)}, f32[272,2176]{1,0:T(8,128)}, u32[]{:S(2)}) copy-start(f32[272,2176]{1,0:T(8,128)} %get-tuple-element.15) | copy-start | bytes 7102468
  203.2 1.3 copy-start.10
  206.5 34.3 %copy-start.1 = (f32[16,128,128]{2,1,0:T(8,128)S(1)}, f32[16,128,128]{2,1,0:T(8,128)}, u32[]{:S(2)}) copy-start(f32[16,128,128]{2,1,0:T(8,128)} %param.14) | copy-start | bytes 3145732

commit v3 on v2

--- a/solution.py
+++ b/solution.py
@@ -216,6 +216,17 @@
     )(terms, band)
 
 
+def extended(cells, sides, width):
+    for axis, dim in sides:
+        ends = lax.axis_size(axis) - 1
+        head = lax.slice_in_dim(cells, 0, width, axis=dim)
+        tail = lax.slice_in_dim(cells, cells.shape[dim] - width, cells.shape[dim], axis=dim)
+        before = lax.ppermute(tail, axis, [(i, i + 1) for i in range(ends)])
+        after = lax.ppermute(head, axis, [(i + 1, i) for i in range(ends)])
+        cells = jnp.concatenate([before, cells, after], axis=dim)
+    return cells
+
+
 def band_weights(headings, extents):
     shape = (3, 2, TILE_ROWS, TILE_LANES, TILE_ROWS, TILE_LANES)
     index = [lax.broadcasted_iota(jnp.int32, shape, axis) for axis in range(6)]
@@ -254,18 +265,13 @@
     window_rows = side_cells // row_count
     window_columns = side_cells // (col_count * split)
 
-    tiles_down, tiles_over = tile_choice_index.shape
-    told = jnp.concatenate(
-        [tile_choice_index.reshape(-1), family_heading_index, family_extent_index]
-    )
-    told = lax.all_gather(told, ("row", "col", "orient"))
-    told = told.reshape(row_count, col_count, split, told.shape[1])
-    noise, told = lax.optimization_barrier((noise, told))
-    area = tiles_down * tiles_over
-    choices = told[:, :, 0, :area].reshape(row_count, col_count, tiles_down, tiles_over)
-    choices = choices.transpose(0, 2, 1, 3).reshape(row_count * tiles_down, col_count * tiles_over)
-    families = told[0, 0, :, area:].reshape(split, 2, -1)
-    families = families.transpose(1, 0, 2).reshape(2, -1)
+    families = jnp.stack([family_heading_index, family_extent_index])
+    held_families = [families]
+    for turn in range(1, split):
+        pairs = [(i, (i + turn) % split) for i in range(split)]
+        held_families.append(lax.ppermute(families, "orient", pairs))
+    families = jnp.concatenate(held_families, axis=1)
+    choices = extended(tile_choice_index, (("row", 0), ("col", 1)), 1)
 
     own = lax.dynamic_slice_in_dim(noise, side * lines, lines, 1)
     first_line = lax.axis_index(("row", "col", "orient")) * lines
@@ -273,6 +279,7 @@
     u_index = lax.broadcasted_iota(jnp.int32, (lines, side_cells), 1)
     weights = own * amplitude(u_index, v_index, side_cells)[None]
     spectrum = transform(weights, False, lines, side_cells, devices, 0)
+    spectrum, choices, families = lax.optimization_barrier((spectrum, choices, families))
     held = lax.all_to_all(spectrum, ("row", "col", "orient"), split_axis=0, concat_axis=0, tiled=True)
     tall = window_columns + 2 * R
     wide = (window_rows // LANES + 1) * LANES
@@ -281,10 +288,7 @@
     tiles_x = window_rows // tile_side
     tiles_y = window_columns // tile_side
     first_y = col * split + side
-    padded_choices = jnp.pad(choices, 1)
-    local = lax.dynamic_slice(
-        padded_choices, (row * tiles_x, first_y * tiles_y), (tiles_x + 2, tiles_y + 2)
-    )
+    local = lax.dynamic_slice_in_dim(choices, side * tiles_y, tiles_y + 2, 1)
     slope = jnp.take(elevation_library.transpose(0, 2, 1), local.T, axis=0, mode="clip")
     slope = slope.transpose(0, 2, 1, 3).reshape((tiles_y + 2) * tile_side, (tiles_x + 2) * tile_side)
     edge = tile_side - R
@@ -297,7 +301,7 @@
     grip = jnp.where(inside, 0.6 / secant, 0.0)
     drive = jnp.where(inside, slope / secant, 0.0).astype(jnp.bfloat16)
     band = band_weights(families[0], families[1])
-    held, lift, grip, drive, band = lax.optimization_barrier((held, lift, grip, drive, band))
+    held, lift, grip, drive = lax.optimization_barrier((held, lift, grip, drive))
     positions = side_cells // devices
     per_block = LANES // lines
     held = held.reshape(side_cells // LANES, per_block, 2, positions, lines)

time: 244 us -> 204 us (0.84)
  blocking collectives: 96.7 us -> 0 us
  waiting for transfers between devices: 5.14 us -> 53.4 us
  starting transfers between devices: 9.4 us -> 31.2 us
  local copies, waits for them, and re-layouts: 55.5 us -> 41.5 us
    all_to_all x1 -> x0, blocking collectives: 57.1 us -> none  [body(): lax.all_to_all(fields, ('col', 'orient'), split_axis=0, concat_axis=0, ti...]
    unnamed x1 -> x0, blocking collectives: 39.6 us -> none
    all_to_all x0 -> x1, waiting for transfers between devices: none -> 28.3 us  [body(): lax.all_to_all(fields, ('col', 'orient'), split_axis=0, concat_axis=0, ti...]
    all_to_all x1, waiting for transfers between devices: 0.01 us -> 24.5 us  [body(): lax.all_to_all(spectrum, ('row', 'col', 'orient'), split_axis=0, concat_a...]
    ppermute x0 -> x5, starting transfers between devices: none -> 10.8 us  [the longest x2 5.23 us: extended(): after = lax.ppermute(head, axis, [(i + 1, i) for i in range(ends)])]
    all_to_all x0 -> x1, starting transfers between devices: none -> 8.08 us  [body(): lax.all_to_all(fields, ('col', 'orient'), split_axis=0, concat_axis=0, ti...]
    ppermute x1, waiting for transfers between devices: 3.8 us -> 0.01 us  [body(): lax.ppermute(fields[:, :, window_rows - R:], 'row', [(i, i + 1) for i in...]
    broadcast_in_dim x2, local copies, waits for them, and re-layouts: 4.49 us -> 1.24 us  [whole(): jnp.where(keep, cells, 0.0).astype(jnp.bfloat16)]
  transfers between devices with their start and end apart: 3 -> 9, of which waited for: 2 -> 3; matrix products, arithmetic and copies ran while one was open for 25% -> 26% of each run, Pallas kernels for 0% -> 4%
where the time goes in v3:
time: 204 us; the launch traced here: 202 us
  waiting for transfers between devices  53.4 us (26%)
  Pallas kernels  49 us (24%)
  local copies, waits for them, and re-layouts  41.5 us (20%)
  starting transfers between devices  31.2 us (15%)
  other arithmetic  26.5 us (13%)
    pallas_call x1, Pallas kernels, stability(): pl.pallas_call(functools.partial(stability_kernel, families), grid=(heigh...  31.5 us
    all_to_all x1, waiting for transfers between devices, body(): lax.all_to_all(fields, ('col', 'orient'), split_axis=0, concat_axis=0, ti...  28.3 us
    all_to_all x1, waiting for transfers between devices, body(): lax.all_to_all(spectrum, ('row', 'col', 'orient'), split_axis=0, concat_a...  24.5 us
    pallas_call x2, Pallas kernels, transform(): pl.pallas_call(functools.partial(transform_kernel, planes, blocks, span,...  17.6 us
    mul x5, local copies, waits for them, and re-layouts, ellipsoid(): along = offset_u * jnp.cos(heading) + offset_v * jnp.sin(heading)  13 us
    gather x2, local copies, waits for them, and re-layouts, body(): jnp.take(elevation_library.transpose(0, 2, 1), local.T, axis=0, mode='clip')  8.66 us
    all_to_all x1, starting transfers between devices, body(): lax.all_to_all(fields, ('col', 'orient'), split_axis=0, concat_axis=0, ti...  8.08 us
    convert_element_type x2, other arithmetic, whole(): jnp.where(keep, cells, 0.0).astype(jnp.bfloat16)  7.34 us
  transfers between devices with their start and end apart: 9, of which 3 were waited for; matrix products, arithmetic and copies ran while one was open for 26% of the time, Pallas kernels for 4%

profile of v3, /device:TPU:13, one launch (start us, length us, event | category | flops | bytes accessed | tf_op | source)
XLA Modules:
  0.0 201.9 jit_solution(269211810939347296)
XLA Ops:
  7.7 2.7 %dynamic-slice_multiply_fusion.in_ref = f32[2,128,4096]{2,1,0:T(8,128)S(1)} fusion(f32[2,256,4096]{2,1,0:T(8,128)} %param.13, s32[]{:T(128)S(6)} %select_n.37, f32[128,4096]{1,0:T(8,128)S(1)} %fusion.11), kind=kLoop, calls=%fused_computation.3 | loop fusion | flops 1048576 | bytes 10485764 | tf_op jit(solution)/shard_map/mul | solution.py:280
  10.5 8.6 %shard_map.127 = bf16[32,2,128,128]{3,2,1,0:T(8,128)(2,1)} custom-call(f32[2,128,4096]{2,1,0:T(8,128)S(1)} %dynamic-slice_multiply_fusion.in_ref, f32[32,128]{1,0:T(8,128)S(1)} %copy-done.4, f32[32,128]{1,0:T(8,128)S(1)} %copy-done.5, bf16[256,256]{1,0:T(8,128)(2,1)S(1)} %copy-done.2, bf16[256,256]{1,0:T(8,128)(2,1)S(1)} %copy-done.3), custom_call_target="tpu_custom_call" | custom-call | tf_op jit(solution)/shard_map/pallas_call | solution.py:132
  19.2 3.1 %collective-permute-start.3 = (s32[18,1]{0,1:T(1,128)S(1)}, s32[18,1]{0,1:T(1,128)S(1)}, u32[]{:S(2)}, u32[]{:S(2)}) collective-permute-start(s32[18,1]{0,1:T(1,128)S(1)} %get-tuple-element.29), channel_id=1, source_target_pairs={{2,0},{4,2},{6,4},{8,6},{10,8},{12,10},{14,12},{3,1},{5,3},{7,5},{... | collective-permute-start | bytes 224 | tf_op jit(solution)/shard_map/ppermute | solution.py:225
  22.3 3.1 %collective-permute-start.2 = (s32[18,1]{0,1:T(1,128)S(1)}, s32[18,1]{0,1:T(1,128)S(1)}, u32[]{:S(2)}, u32[]{:S(2)}) collective-permute-start(s32[18,1]{0,1:T(1,128)S(1)} %get-tuple-element.28), channel_id=1, source_target_pairs={{0,2},{2,4},{4,6},{6,8},{8,10},{10,12},{12,14},{1,3},{3,5},{5,7},{... | collective-permute-start | bytes 224 | tf_op jit(solution)/shard_map/ppermute | solution.py:224
  26.2 6.9 %all-to-all-start = ((bf16[32,2,128,128]{3,2,1,0:T(8,128)(2,1)}), bf16[32,2,128,128]{3,2,1,0:T(8,128)(2,1)S(1)}, u32[]{:S(2)}, u32[]{:S(2)}) async-start(bf16[32,2,128,128]{3,2,1,0:T(8,128)(2,1)} %shard_map.127), calls=%async_computation | async-start | bytes 4194304 | tf_op jit(solution)/shard_map/all_to_all | solution.py:283
  33.3 3.0 %gather_fusion = f32[72,128,128]{1,2,0:T(8,128)} fusion(f32[16,128,128]{1,2,0:T(8,128)S(1)} %bitcast.66, s32[1024]{0:T(1024)S(1)} %pad_clamp_fusion), kind=kCustom, calls=%fused_computation | custom fusion | bytes 9437472 | tf_op jit(solution)/shard_map/jit(_take)/gather | solution.py:292
  36.3 5.7 %copy.17 = f32[4,18,128,128]{2,0,3,1:T(4,128)S(1)} copy(f32[4,18,128,128]{2,3,1,0:T(8,128)} %bitcast.67) | data formatting | bytes 9437184 | tf_op jit(solution)/shard_map/jit(_take)/gather | solution.py:292
  42.5 2.6 %slice.46 = f32[272,2176]{0,1:T(8,128)} slice(f32[512,2304]{0,1:T(8,128)S(1)} %bitcast.69), slice={[120:392], [120:2296]} | slice | bytes 4734976 | tf_op jit(solution)/shard_map/slice | solution.py:295
  45.1 3.5 %copy.21 = f32[272,2176]{1,0:T(8,128)} copy(f32[272,2176]{0,1:T(8,128)} %slice.46) | data formatting | bytes 4734976
  48.6 5.8 %select_convert_fusion.2 = (bf16[272,2176]{1,0:T(8,128)(2,1)}, f32[272,2176]{1,0:T(8,128)}, f32[272,2176]{1,0:T(8,128)}) fusion(f32[272,2176]{1,0:T(8,128)} %copy.21, pred[2176]{0:T(1024)(128)(4,1)S(1)} %get-tuple-element.37, pred[2176]{0:T(1024)(128)(4,1)S(1)} %get-tuple-element.38, pred[272]{0:T(512)(128)(4,1)S(1)} %fusion.25), kind=kLoop, calls=%fused_computation.19 | loop fusion | flops 6510592 | bytes 8290832 | tf_op jit(solution)/shard_map/convert_element_type | solution.py:302
  54.4 24.5 %all-to-all-done.in_ref = bf16[32,2,128,128]{3,2,1,0:T(8,128)(2,1)S(1)} async-done(((bf16[32,2,128,128]{3,2,1,0:T(8,128)(2,1)}), bf16[32,2,128,128]{3,2,1,0:T(8,128)(2,1)S(1)}, u32[]{:S(2)}, u32[]{:S(2)}) %all-to-all-start) | async-done | bytes 2097184 | tf_op jit(solution)/shard_map/all_to_all | solution.py:283
  78.9 9.0 %shard_map.128 = bf16[16,2,272,128]{3,2,1,0:T(8,128)(2,1)} custom-call(bf16[32,2,128,128]{3,2,1,0:T(8,128)(2,1)S(1)} %all-to-all-done.in_ref, f32[32,128]{1,0:T(8,128)S(1)} %copy-done.4, f32[32,128]{1,0:T(8,128)S(1)} %copy-done.5, bf16[256,256]{1,0:T(8,128)(2,1)S(1)} %copy-done.2, bf16[256,256]{1,0:T(8,128)(2,1)S(1)} %copy-done.3), custom_call_target="tpu_custom_call" | custom-call | tf_op jit(solution)/shard_map/pallas_call | solution.py:132
  87.9 8.1 %all-to-all-start.1 = ((bf16[16,2,272,128]{3,2,1,0:T(8,128)(2,1)}), bf16[16,2,272,128]{3,2,1,0:T(8,128)(2,1)}, u32[]{:S(2)}, u32[]{:S(2)}) async-start(bf16[16,2,272,128]{3,2,1,0:T(8,128)(2,1)} %shard_map.128), calls=%async_computation.1 | async-start | bytes 4456448 | tf_op jit(solution)/shard_map/all_to_all | solution.py:310
  100.1 4.6 %mul.321 = f32[1,3,256,1024]{3,2,1,0:T(8,128)} reshape(f32[768,8,128]{2,1,0:T(8,128)} %mul.320) | data formatting | bytes 6291456 | tf_op jit(solution)/shard_map/mul | solution.py:43
  106.7 4.6 %mul.328 = f32[1,3,256,1024]{3,2,1,0:T(8,128)} reshape(f32[768,8,128]{2,1,0:T(8,128)} %mul.327) | data formatting | bytes 6291456 | tf_op jit(solution)/shard_map/mul | solution.py:43
  111.5 4.7 %select_convert_fusion.1 = (bf16[1,3,256,1024]{3,2,1,0:T(8,128)(2,1)}, f32[1,3,256,1024]{3,2,1,0:T(8,128)S(1)}) fusion(pred[1,3,256,1024]{3,2,1,0:T(8,128)(4,1)S(1)} %broadcast_in_dim.38, f32[1024]{0:T(1024)S(1)} %get-tuple-element.40, f32[1,3,256,1024]{3,2,1,0:T(8,128)} %mul.321, f32[1,3,256,1024]{3,2,1,0:T(8,128)} %mul.328, f32[1024]{0:T(1024)S(1)} %get-tuple-element.41, ...), kind=kLoop, calls=%fused_computation.6 | loop fusion | flops 12582912 | bytes 11812864 | tf_op jit(solution)/shard_map/convert_element_type | solution.py:251
  116.3 2.6 %select_convert_fusion = bf16[1,3,256,1024]{3,2,1,0:T(8,128)(2,1)} fusion(pred[1,3,256,1024]{3,2,1,0:T(8,128)(4,1)S(1)} %broadcast_in_dim.38, f32[1,3,256,1024]{3,2,1,0:T(8,128)S(1)} %get-tuple-element.20, f32[1024]{0:T(1024)S(1)} %get-tuple-element.39), kind=kLoop, calls=%fused_computation.5 | loop fusion | flops 3145728 | bytes 5509120 | tf_op jit(solution)/shard_map/convert_element_type | solution.py:251
  118.9 28.3 %all-to-all-done.1 = bf16[16,2,272,128]{3,2,1,0:T(8,128)(2,1)} async-done(((bf16[16,2,272,128]{3,2,1,0:T(8,128)(2,1)}), bf16[16,2,272,128]{3,2,1,0:T(8,128)(2,1)}, u32[]{:S(2)}, u32[]{:S(2)}) %all-to-all-start.1) | async-done | bytes 2228256 | tf_op jit(solution)/shard_map/all_to_all | solution.py:310
  150.7 4.0 %collective-permute-start.6 = (bf16[2,272,8]{2,1,0:T(8,128)(2,1)S(1)}, bf16[2,272,8]{2,1,0:T(8,128)(2,1)S(1)}, u32[]{:S(2)}, u32[]{:S(2)}) collective-permute-start(bf16[2,272,8]{2,1,0:T(8,128)(2,1)S(1)} %get-tuple-element.26), channel_id=1, source_target_pairs={{16,0},{17,1},{18,2},{19,3},{20,4},{21,5},{22,6},{23,7},{24,8},{25... | collective-permute-start | bytes 26120 | tf_op jit(solution)/shard_map/ppermute | solution.py:314
  154.7 2.5 %pad_maximum_fusion.band_ref = bf16[3,3,256,1024]{3,2,1,0:T(8,128)(2,1)} fusion(bf16[1,3,256,1024]{3,2,1,0:T(8,128)(2,1)S(1)} %copy-done.8, bf16[1,3,256,1024]{3,2,1,0:T(8,128)(2,1)S(1)} %copy-done.9), kind=kLoop, calls=%fused_computation.2 | loop fusion | flops 4718592 | bytes 7864320 | tf_op jit(solution)/shard_map/stack | solution.py:254
  157.2 4.0 %concatenate.15 = bf16[2,272,2176]{2,1,0:T(8,128)(2,1)} concatenate(bf16[2,272,8]{2,1,0:T(8,128)(2,1)S(1)} %collective-permute-done.5, bf16[2,272,2048]{2,1,0:T(8,128)(2,1)S(1)} %copy_bitcast_fusion.1, bf16[2,272,8]{2,1,0:T(8,128)(2,1)S(1)} %collective-permute-done.6, bf16[2,272,112]{2,1,0:T(8,128)(2,1)S(1)} %broadcast_in_dim.36), dimensions={2} | concatenate | bytes 4734976 | tf_op jit(solution)/shard_map/concatenate | solution.py:315
  161.2 2.1 %convert_element_type.90 = f32[2,272,2176]{2,1,0:T(8,128)S(1)} convert(bf16[2,272,2176]{2,1,0:T(8,128)(2,1)} %concatenate.15) | non-fusion elementwise | flops 1183744 | bytes 7102464 | tf_op jit(solution)/shard_map/convert_element_type | solution.py:317
  167.6 31.5 %shard_map.129 = f32[256,2048]{1,0:T(8,128)} custom-call(bf16[3,272,2176]{2,1,0:T(8,128)(2,1)} %pad_maximum_fusion.1.term_ref, bf16[3,3,256,1024]{3,2,1,0:T(8,128)(2,1)} %pad_maximum_fusion.band_ref), custom_call_target="tpu_custom_call" | custom-call | tf_op jit(solution)/shard_map/pallas_call | solution.py:202
  199.0 2.9 %copy.20 = f32[2048,256]{1,0:T(8,128)} copy(f32[2048,256]{0,1:T(8,128)} %bitcast.70) | data formatting | bytes 4194304 | tf_op jit(solution)/shard_map/transpose | solution.py:322
  (81 shorter events, 23.3 us)
Async XLA Ops:
  0.0 33.3 %copy-start = (f32[16,128,128]{2,1,0:T(8,128)S(1)}, f32[16,128,128]{2,1,0:T(8,128)}, u32[]{:S(2)}) copy-start(f32[16,128,128]{2,1,0:T(8,128)} %param.14) | copy-start | bytes 3145732
  0.9 18.2 %collective-permute-start.1 = (s32[1,4]{0,1:T(4,128)S(1)}, s32[1,4]{0,1:T(4,128)S(1)}, u32[]{:S(2)}, u32[]{:S(2)}) collective-permute-start(s32[1,4]{0,1:T(4,128)S(1)} %get-tuple-element.31), channel_id=1, source_target_pairs={{16,0},{17,1},{18,2},{19,3},{20,4},{21,5},{22,6},{23,7},{24,8},{25... | collective-permute-start | bytes 56 | tf_op jit(solution)/shard_map/ppermute | solution.py:225
  3.0 16.1 %collective-permute-start = (s32[1,4]{0,1:T(4,128)S(1)}, s32[1,4]{0,1:T(4,128)S(1)}, u32[]{:S(2)}, u32[]{:S(2)}) collective-permute-start(s32[1,4]{0,1:T(4,128)S(1)} %get-tuple-element.30), channel_id=1, source_target_pairs={{0,16},{1,17},{2,18},{3,19},{4,20},{5,21},{6,22},{7,23},{8,24},{9,... | collective-permute-start | bytes 56 | tf_op jit(solution)/shard_map/ppermute | solution.py:224
  5.0 20.4 %collective-permute-start.4 = (s32[2,4]{1,0:T(2,128)S(1)}, s32[2,4]{1,0:T(2,128)S(1)}, u32[]{:S(2)}, u32[]{:S(2)}) collective-permute-start(s32[2,4]{1,0:T(2,128)S(1)} %pad_add_fusion.2), channel_id=1, source_target_pairs={{0,1},{1,0},{2,3},{3,2},{4,5},{5,4},{6,7},{7,6},{8,9},{9,8},{10,11... | collective-permute-start | bytes 104 | tf_op jit(solution)/shard_map/ppermute | solution.py:272
  7.6 2.8 %copy-start.2 = (bf16[256,256]{1,0:T(8,128)(2,1)S(1)}, bf16[256,256]{1,0:T(8,128)(2,1)}, u32[]{:S(2)}) copy-start(bf16[256,256]{1,0:T(8,128)(2,1)} %constant.89.clone.big_ref) | copy-start | bytes 393220
  7.6 2.8 %copy-start.3 = (bf16[256,256]{1,0:T(8,128)(2,1)S(1)}, bf16[256,256]{1,0:T(8,128)(2,1)}, u32[]{:S(2)}) copy-start(bf16[256,256]{1,0:T(8,128)(2,1)} %constant.90.clone.small_ref) | copy-start | bytes 393220
  7.7 2.8 %copy-start.4 = (f32[32,128]{1,0:T(8,128)S(1)}, f32[32,128]{1,0:T(8,128)}, u32[]{:S(2)}) copy-start(f32[32,128]{1,0:T(8,128)} %constant.87.clone.cos_ref) | copy-start | bytes 49156
  7.7 2.8 %copy-start.5 = (f32[32,128]{1,0:T(8,128)S(1)}, f32[32,128]{1,0:T(8,128)}, u32[]{:S(2)}) copy-start(f32[32,128]{1,0:T(8,128)} %constant.88.clone.sin_ref) | copy-start | bytes 49156
  10.5 8.6 %copy-start.11 = (s32[16,4]{0,1:T(4,128)S(1)}, s32[16,4]{0,1:T(4,128)}, u32[]{:S(2)}) copy-start(s32[16,4]{0,1:T(4,128)} %param.15) | copy-start | bytes 772
  10.5 14.9 %copy-start.12 = (s32[4]{0:T(128)S(1)}, s32[4]{0:T(128)}, u32[]{:S(2)}) copy-start(s32[4]{0:T(128)} %param.17) | copy-start | bytes 52
  10.5 14.9 %copy-start.13 = (s32[4]{0:T(128)S(1)}, s32[4]{0:T(128)}, u32[]{:S(2)}) copy-start(s32[4]{0:T(128)} %param.16) | copy-start | bytes 52
  19.2 6.3 %collective-permute-start.3 = (s32[18,1]{0,1:T(1,128)S(1)}, s32[18,1]{0,1:T(1,128)S(1)}, u32[]{:S(2)}, u32[]{:S(2)}) collective-permute-start(s32[18,1]{0,1:T(1,128)S(1)} %get-tuple-element.29), channel_id=1, source_target_pairs={{2,0},{4,2},{6,4},{8,6},{10,8},{12,10},{14,12},{3,1},{5,3},{7,5},{... | collective-permute-start | bytes 224 | tf_op jit(solution)/shard_map/ppermute | solution.py:225
  22.3 3.8 %collective-permute-start.2 = (s32[18,1]{0,1:T(1,128)S(1)}, s32[18,1]{0,1:T(1,128)S(1)}, u32[]{:S(2)}, u32[]{:S(2)}) collective-permute-start(s32[18,1]{0,1:T(1,128)S(1)} %get-tuple-element.28), channel_id=1, source_target_pairs={{0,2},{2,4},{4,6},{6,8},{8,10},{10,12},{12,14},{1,3},{3,5},{5,7},{... | collective-permute-start | bytes 224 | tf_op jit(solution)/shard_map/ppermute | solution.py:224
  26.2 52.7 %all-to-all-start = ((bf16[32,2,128,128]{3,2,1,0:T(8,128)(2,1)}), bf16[32,2,128,128]{3,2,1,0:T(8,128)(2,1)S(1)}, u32[]{:S(2)}, u32[]{:S(2)}) async-start(bf16[32,2,128,128]{3,2,1,0:T(8,128)(2,1)} %shard_map.127), calls=%async_computation | async-start | bytes 4194304 | tf_op jit(solution)/shard_map/all_to_all | solution.py:283
  87.9 59.3 %all-to-all-start.1 = ((bf16[16,2,272,128]{3,2,1,0:T(8,128)(2,1)}), bf16[16,2,272,128]{3,2,1,0:T(8,128)(2,1)}, u32[]{:S(2)}, u32[]{:S(2)}) async-start(bf16[16,2,272,128]{3,2,1,0:T(8,128)(2,1)} %shard_map.128), calls=%async_computation.1 | async-start | bytes 4456448 | tf_op jit(solution)/shard_map/all_to_all | solution.py:310
  147.2 7.5 %copy-start.8 = (bf16[1,3,256,1024]{3,2,1,0:T(8,128)(2,1)S(1)}, bf16[1,3,256,1024]{3,2,1,0:T(8,128)(2,1)}, u32[]{:S(2)}) copy-start(bf16[1,3,256,1024]{3,2,1,0:T(8,128)(2,1)} %select_convert_fusion) | copy-start | bytes 4718596
  147.2 7.5 %copy-start.9 = (bf16[1,3,256,1024]{3,2,1,0:T(8,128)(2,1)S(1)}, bf16[1,3,256,1024]{3,2,1,0:T(8,128)(2,1)}, u32[]{:S(2)}) copy-start(bf16[1,3,256,1024]{3,2,1,0:T(8,128)(2,1)} %get-tuple-element.19) | copy-start | bytes 4718596
  149.4 7.8 %collective-permute-start.5 = (bf16[2,272,8]{2,1,0:T(8,128)(2,1)S(1)}, bf16[2,272,8]{2,1,0:T(8,128)(2,1)S(1)}, u32[]{:S(2)}, u32[]{:S(2)}) collective-permute-start(bf16[2,272,8]{2,1,0:T(8,128)(2,1)S(1)} %get-tuple-element.27), channel_id=1, source_target_pairs={{0,16},{1,17},{2,18},{3,19},{4,20},{5,21},{6,22},{7,23},{8,24},{9,... | collective-permute-start | bytes 26120 | tf_op jit(solution)/shard_map/ppermute | solution.py:313
  150.7 6.5 %collective-permute-start.6 = (bf16[2,272,8]{2,1,0:T(8,128)(2,1)S(1)}, bf16[2,272,8]{2,1,0:T(8,128)(2,1)S(1)}, u32[]{:S(2)}, u32[]{:S(2)}) collective-permute-start(bf16[2,272,8]{2,1,0:T(8,128)(2,1)S(1)} %get-tuple-element.26), channel_id=1, source_target_pairs={{16,0},{17,1},{18,2},{19,3},{20,4},{21,5},{22,6},{23,7},{24,8},{25... | collective-permute-start | bytes 26120 | tf_op jit(solution)/shard_map/ppermute | solution.py:314
  161.2 2.4 %copy-start.6 = (f32[272,2176]{1,0:T(8,128)S(1)}, f32[272,2176]{1,0:T(8,128)}, u32[]{:S(2)}) copy-start(f32[272,2176]{1,0:T(8,128)} %get-tuple-element.16) | copy-start | bytes 7102468
  161.2 3.1 %copy-start.7 = (f32[272,2176]{1,0:T(8,128)S(1)}, f32[272,2176]{1,0:T(8,128)}, u32[]{:S(2)}) copy-start(f32[272,2176]{1,0:T(8,128)} %get-tuple-element.15) | copy-start | bytes 7102468
  164.3 1.3 copy-start.10
  167.6 34.4 %copy-start.1 = (f32[16,128,128]{2,1,0:T(8,128)S(1)}, f32[16,128,128]{2,1,0:T(8,128)}, u32[]{:S(2)}) copy-start(f32[16,128,128]{2,1,0:T(8,128)} %param.14) | copy-start | bytes 3145732

commit v4 on v3

--- a/solution.py
+++ b/solution.py
@@ -151,9 +151,8 @@
     return jnp.take_along_axis(level, 7 - row, axis=1)
 
 
-def stability_kernel(families, term_ref, band_ref, out_ref, swapped, gathered):
-    tiles = gathered.shape[1]
-    across = gathered.shape[2]
+def gather_tiles(term_ref, swapped, gathered):
+    tiles, across = gathered.shape[1:3]
     chunks = across // GROUPS
 
     @pl.when(pl.program_id(0) == 0)
@@ -161,32 +160,44 @@
         @pl.loop(0, tiles // 2)
         def _(pair):
             at = pl.ds(pl.multiple_of(pair * 16, 16), 16)
-            for term in range(3):
+            both = pl.ds(pair * 2, 2)
+            for term in range(gathered.shape[0]):
                 for chunk in range(chunks + 1):
                     cells = term_ref[term, at, chunk * LANES : (chunk + 1) * LANES].astype(jnp.float32)
                     turned = swap_groups(cells.reshape(2, TILE_ROWS, LANES))
                     swapped[:, chunk * GROUPS : (chunk + 1) * GROUPS, :] = turned
-                both = pl.ds(pair * 2, 2)
                 gathered[term, both, :, 0:PHASE] = swapped[:, 0:across, :].astype(jnp.bfloat16)
                 gathered[term, both, :, PHASE:] = swapped[:, 1 : across + 1, :].astype(jnp.bfloat16)
 
+
+def column_sum(gathered, band_ref, lanes):
+    terms, _, across, depth = gathered.shape
     tile = pl.program_id(0) * STEP_TILES
+    pieces = [(term, shift) for term in range(terms) for shift in range(3)]
+    left = [gathered[term, pl.ds(tile + shift, STEP_TILES)] for term, shift in pieces]
+    left = [piece.reshape(STEP_TILES * across, depth) for piece in left]
+    right = [band_ref[term, shift, :, lanes] for term, shift in pieces]
+    return jnp.dot(
+        jnp.concatenate(left, axis=1),
+        jnp.concatenate(right, axis=0),
+        preferred_element_type=jnp.float32,
+    )
+
+
+def driving_kernel(families, term_ref, band_ref, out_ref, swapped, gathered):
+    gather_tiles(term_ref, swapped, gathered)
+    for pair in range(families // 2):
+        lanes = slice(pair * 2 * PHASE, (pair + 1) * 2 * PHASE)
+        out_ref[:, lanes] = column_sum(gathered, band_ref, lanes)
+
+
+def stability_kernel(families, term_ref, band_ref, drive_ref, out_ref, swapped, gathered):
+    chunks = gathered.shape[2] // GROUPS
+    gather_tiles(term_ref, swapped, gathered)
     low = None
     for pair in range(families // 2):
         lanes = slice(pair * 2 * PHASE, (pair + 1) * 2 * PHASE)
-
-        def total(chosen):
-            pieces = [(term, shift) for term in chosen for shift in range(3)]
-            left = [gathered[term, pl.ds(tile + shift, STEP_TILES)] for term, shift in pieces]
-            left = [piece.reshape(STEP_TILES * across, 2 * PHASE) for piece in left]
-            right = [band_ref[term, shift, :, lanes] for term, shift in pieces]
-            return jnp.dot(
-                jnp.concatenate(left, axis=1),
-                jnp.concatenate(right, axis=0),
-                preferred_element_type=jnp.float32,
-            )
-
-        ratio = total((0, 1)) / total((2,))
+        ratio = column_sum(gathered, band_ref, lanes) / drive_ref[:, lanes]
         least = jnp.minimum(ratio[:, 0:PHASE], ratio[:, PHASE:])
         low = least if low is None else jnp.minimum(low, least)
     turned = swap_groups(low.reshape(STEP_TILES * chunks, TILE_ROWS, LANES))
@@ -195,25 +206,29 @@
             out_ref[side * 8 : side * 8 + 8, chunk * LANES : (chunk + 1) * LANES] = turned[side * chunks + chunk]
 
 
-def stability(terms, band, height, width):
+def tile_call(kernel, terms, band, height, width, out_shape, out_block, more=()):
     families = band.shape[-1] // PHASE
     across = width // TILE_LANES
     tiles = height // TILE_ROWS + 2
+    count = terms.shape[0]
+    work = 2 * (height // TILE_ROWS) * across * band.size
     return pl.pallas_call(
-        functools.partial(stability_kernel, families),
+        functools.partial(kernel, families),
         grid=(height // (TILE_ROWS * STEP_TILES),),
-        out_shape=jax.ShapeDtypeStruct((height, width), jnp.float32),
+        out_shape=jax.ShapeDtypeStruct(out_shape, jnp.float32),
         in_specs=[
             pl.BlockSpec(terms.shape, lambda i: (0, 0, 0), pipeline_mode=pl.Buffered(1)),
             pl.BlockSpec(band.shape, lambda i: (0, 0, 0, 0), pipeline_mode=pl.Buffered(1)),
-        ],
-        out_specs=pl.BlockSpec((TILE_ROWS * STEP_TILES, width), lambda i: (i, 0)),
+        ]
+        + [pl.BlockSpec((STEP_TILES * across, cells.shape[1]), lambda i: (i, 0)) for cells in more],
+        out_specs=pl.BlockSpec(out_block, lambda i: (i, 0)),
         scratch_shapes=[
             pltpu.VMEM((2, across + GROUPS, LANES), jnp.float32),
-            pltpu.VMEM((3, tiles, across, 2 * PHASE), jnp.bfloat16),
+            pltpu.VMEM((count, tiles, across, 2 * PHASE), jnp.bfloat16),
         ],
         compiler_params=pltpu.CompilerParams(vmem_limit_bytes=56 << 20),
-    )(terms, band)
+        cost_estimate=pl.CostEstimate(flops=work, bytes_accessed=16 << 20, transcendentals=0),
+    )(terms, band, *more)
 
 
 def extended(cells, sides, width):
@@ -251,7 +266,7 @@
         return jnp.where(keep, cells, 0.0).astype(jnp.bfloat16).reshape(3, 2 * PHASE, count * PHASE)
 
     heights = whole(heights)
-    return jnp.stack([whole(shares), heights, heights])
+    return jnp.stack([whole(shares), heights])
 
 
 def body(noise, elevation_library, tile_choice_index, family_heading_index, family_extent_index):
@@ -308,6 +323,17 @@
     held = held.transpose(0, 2, 3, 1, 4).reshape(side_cells // LANES, 2, positions, LANES)
     fields = transform(held, True, positions, side_cells, col_count * split, R)
     fields = lax.all_to_all(fields, ("col", "orient"), split_axis=0, concat_axis=0, tiled=True)
+    across = window_rows // TILE_LANES
+    driving = tile_call(
+        driving_kernel,
+        drive[None],
+        band[1:],
+        window_columns,
+        window_rows,
+        (window_columns // TILE_ROWS * across, band.shape[-1]),
+        (STEP_TILES * across, band.shape[-1]),
+    )
+    fields, driving, band = lax.optimization_barrier((fields, driving, band))
     fields = fields.transpose(1, 2, 0, 3).reshape(2, tall, window_rows)
     ends = row_count - 1
     before = lax.ppermute(fields[:, :, window_rows - R :], "row", [(i, i + 1) for i in range(ends)])
@@ -318,8 +344,17 @@
 
     cohesion = (jnp.exp(0.4 * fields[0]) * lift).astype(jnp.bfloat16)
     friction = (jnp.exp(0.25 * fields[1]) * grip).astype(jnp.bfloat16)
-    terms = jnp.stack([cohesion, friction, drive])
-    return stability(terms, band, window_columns, window_rows).T
+    safety = tile_call(
+        stability_kernel,
+        jnp.stack([cohesion, friction]),
+        band,
+        window_columns,
+        window_rows,
+        (window_columns, window_rows),
+        (TILE_ROWS * STEP_TILES, window_rows),
+        (driving,),
+    )
+    return safety.T
 
 
 def solution(mesh):

time: 204 us -> 196 us (0.961)
  waiting for transfers between devices: 53.4 us -> 46.2 us
  Pallas kernels: 49 us -> 55 us
  other arithmetic: 26.5 us -> 23.8 us
  starting transfers between devices: 31.2 us -> 28.9 us
    all_to_all x1, waiting for transfers between devices: 28.3 us -> 14 us  [body(): lax.all_to_all(fields, ('col', 'orient'), split_axis=0, concat_axis=0, ti...]
    pallas_call x1 -> x2, Pallas kernels: 31.5 us -> 37.4 us  [tile_call(): pl.pallas_call(functools.partial(kernel, families), grid=(height // (TILE...]
    ppermute x1, waiting for transfers between devices: 0.01 us -> 4.1 us  [body(): lax.ppermute(fields[:, :, window_rows - R:], 'row', [(i, i + 1) for i in...]
    all_to_all x1, starting transfers between devices: 6.95 us -> 3.83 us  [body(): lax.all_to_all(spectrum, ('row', 'col', 'orient'), split_axis=0, concat_a...]
    ppermute x2, waiting for transfers between devices: 0.01 us -> 2.82 us  [extended(): after = lax.ppermute(head, axis, [(i + 1, i) for i in range(ends)])]
    unnamed x30 -> x26, local copies, waits for them, and re-layouts: 5.49 us -> 5.14 us
  transfers between devices with their start and end apart: 9 -> 9, of which waited for: 3 -> 5; matrix products, arithmetic and copies ran while one was open for 26% -> 25% of each run, Pallas kernels for 4% -> 12%
where the time goes in v4:
time: 196 us; the launch traced here: 195 us
  Pallas kernels  55 us (28%)
  waiting for transfers between devices  46.2 us (24%)
  local copies, waits for them, and re-layouts  41 us (21%)
  starting transfers between devices  28.9 us (15%)
  other arithmetic  23.8 us (12%)
    pallas_call x2, Pallas kernels, tile_call(): pl.pallas_call(functools.partial(kernel, families), grid=(height // (TILE...  37.4 us
    all_to_all x1, waiting for transfers between devices, body(): lax.all_to_all(spectrum, ('row', 'col', 'orient'), split_axis=0, concat_a...  24.4 us
    pallas_call x2, Pallas kernels, transform(): pl.pallas_call(functools.partial(transform_kernel, planes, blocks, span,...  17.5 us
    all_to_all x1, waiting for transfers between devices, body(): lax.all_to_all(fields, ('col', 'orient'), split_axis=0, concat_axis=0, ti...  14 us
    mul x5, local copies, waits for them, and re-layouts, ellipsoid(): along = offset_u * jnp.cos(heading) + offset_v * jnp.sin(heading)  13 us
    gather x2, local copies, waits for them, and re-layouts, body(): jnp.take(elevation_library.transpose(0, 2, 1), local.T, axis=0, mode='clip')  8.67 us
    all_to_all x1, starting transfers between devices, body(): lax.all_to_all(fields, ('col', 'orient'), split_axis=0, concat_axis=0, ti...  8.09 us
    ppermute x2, starting transfers between devices, extended(): after = lax.ppermute(head, axis, [(i + 1, i) for i in range(ends)])  5.9 us
  transfers between devices with their start and end apart: 9, of which 5 were waited for; matrix products, arithmetic and copies ran while one was open for 25% of the time, Pallas kernels for 12%

profile of v4, /device:TPU:13, one launch (start us, length us, event | category | flops | bytes accessed | tf_op | source)
XLA Modules:
  0.0 195.3 jit_solution(7133271090803841562)
XLA Ops:
  4.1 4.0 %collective-permute-start.1 = (s32[1,4]{0,1:T(4,128)S(1)}, s32[1,4]{0,1:T(4,128)S(1)}, u32[]{:S(2)}, u32[]{:S(2)}) collective-permute-start(s32[1,4]{0,1:T(4,128)S(1)} %get-tuple-element.37), channel_id=1, source_target_pairs={{16,0},{17,1},{18,2},{19,3},{20,4},{21,5},{22,6},{23,7},{24,8},{25... | collective-permute-start | bytes 56 | tf_op jit(solution)/shard_map/ppermute | solution.py:240
  9.6 2.7 %dynamic-slice_multiply_fusion.in_ref = f32[2,128,4096]{2,1,0:T(8,128)S(1)} fusion(f32[2,256,4096]{2,1,0:T(8,128)} %param.13, s32[]{:T(128)S(6)} %select_n.37, f32[128,4096]{1,0:T(8,128)S(1)} %fusion.11), kind=kLoop, calls=%fused_computation.2 | loop fusion | flops 1048576 | bytes 10485764 | tf_op jit(solution)/shard_map/mul | solution.py:295
  12.4 8.5 %shard_map.127 = bf16[32,2,128,128]{3,2,1,0:T(8,128)(2,1)} custom-call(f32[2,128,4096]{2,1,0:T(8,128)S(1)} %dynamic-slice_multiply_fusion.in_ref, f32[32,128]{1,0:T(8,128)S(1)} %copy-done.5, f32[32,128]{1,0:T(8,128)S(1)} %copy-done.4, bf16[256,256]{1,0:T(8,128)(2,1)S(1)} %copy-done.3, bf16[256,256]{1,0:T(8,128)(2,1)S(1)} %copy-done.2), custom_call_target="tpu_custom_call" | custom-call | tf_op jit(solution)/shard_map/pallas_call | solution.py:132
  21.1 4.6 %collective-permute-start.2 = (s32[18,1]{0,1:T(1,128)S(1)}, s32[18,1]{0,1:T(1,128)S(1)}, u32[]{:S(2)}, u32[]{:S(2)}) collective-permute-start(s32[18,1]{0,1:T(1,128)S(1)} %get-tuple-element.34), channel_id=1, source_target_pairs={{0,2},{2,4},{4,6},{6,8},{8,10},{10,12},{12,14},{1,3},{3,5},{5,7},{... | collective-permute-start | bytes 224 | tf_op jit(solution)/shard_map/ppermute | solution.py:239
  27.7 2.8 %collective-permute-done.3 = s32[18,1]{0,1:T(1,128)S(1)} collective-permute-done((s32[18,1]{0,1:T(1,128)S(1)}, s32[18,1]{0,1:T(1,128)S(1)}, u32[]{:S(2)}, u32[]{:S(2)}) %collective-permute-start.3) | collective-permute-done | bytes 104 | tf_op jit(solution)/shard_map/ppermute | solution.py:240
  30.6 3.8 %all-to-all-start = ((bf16[32,2,128,128]{3,2,1,0:T(8,128)(2,1)}), bf16[32,2,128,128]{3,2,1,0:T(8,128)(2,1)S(1)}, u32[]{:S(2)}, u32[]{:S(2)}) async-start(bf16[32,2,128,128]{3,2,1,0:T(8,128)(2,1)} %shard_map.127), calls=%async_computation | async-start | bytes 4194304 | tf_op jit(solution)/shard_map/all_to_all | solution.py:298
  34.7 3.0 %gather_fusion = f32[72,128,128]{1,2,0:T(8,128)} fusion(f32[16,128,128]{1,2,0:T(8,128)S(1)} %bitcast.66, s32[1024]{0:T(1024)S(1)} %pad_clamp_fusion), kind=kCustom, calls=%fused_computation | custom fusion | bytes 9437472 | tf_op jit(solution)/shard_map/jit(_take)/gather | solution.py:307
  37.7 5.7 %copy.17 = f32[4,18,128,128]{2,0,3,1:T(4,128)S(1)} copy(f32[4,18,128,128]{2,3,1,0:T(8,128)} %bitcast.67) | data formatting | bytes 9437184 | tf_op jit(solution)/shard_map/jit(_take)/gather | solution.py:307
  43.9 2.6 %slice.46 = f32[272,2176]{0,1:T(8,128)} slice(f32[512,2304]{0,1:T(8,128)S(1)} %bitcast.69), slice={[120:392], [120:2296]} | slice | bytes 4734976 | tf_op jit(solution)/shard_map/slice | solution.py:310
  46.5 3.5 %copy.21 = f32[272,2176]{1,0:T(8,128)} copy(f32[272,2176]{0,1:T(8,128)} %slice.46) | data formatting | bytes 4734976
  50.1 5.8 %select_convert_fusion.2 = (bf16[272,2176]{1,0:T(8,128)(2,1)}, f32[272,2176]{1,0:T(8,128)}, f32[272,2176]{1,0:T(8,128)}) fusion(f32[272,2176]{1,0:T(8,128)} %copy.21, pred[2176]{0:T(1024)(128)(4,1)S(1)} %get-tuple-element.43, pred[2176]{0:T(1024)(128)(4,1)S(1)} %get-tuple-element.44, pred[272]{0:T(512)(128)(4,1)S(1)} %fusion.25), kind=kLoop, calls=%fused_computation.19 | loop fusion | flops 6510592 | bytes 8290832 | tf_op jit(solution)/shard_map/convert_element_type | solution.py:317
  55.9 24.4 %all-to-all-done.in_ref = bf16[32,2,128,128]{3,2,1,0:T(8,128)(2,1)S(1)} async-done(((bf16[32,2,128,128]{3,2,1,0:T(8,128)(2,1)}), bf16[32,2,128,128]{3,2,1,0:T(8,128)(2,1)S(1)}, u32[]{:S(2)}, u32[]{:S(2)}) %all-to-all-start) | async-done | bytes 2097184 | tf_op jit(solution)/shard_map/all_to_all | solution.py:298
  80.2 9.0 %shard_map.128 = bf16[16,2,272,128]{3,2,1,0:T(8,128)(2,1)} custom-call(bf16[32,2,128,128]{3,2,1,0:T(8,128)(2,1)S(1)} %all-to-all-done.in_ref, f32[32,128]{1,0:T(8,128)S(1)} %copy-done.5, f32[32,128]{1,0:T(8,128)S(1)} %copy-done.4, bf16[256,256]{1,0:T(8,128)(2,1)S(1)} %copy-done.3, bf16[256,256]{1,0:T(8,128)(2,1)S(1)} %copy-done.2), custom_call_target="tpu_custom_call" | custom-call | tf_op jit(solution)/shard_map/pallas_call | solution.py:132
  89.2 8.1 %all-to-all-start.1 = ((bf16[16,2,272,128]{3,2,1,0:T(8,128)(2,1)}), bf16[16,2,272,128]{3,2,1,0:T(8,128)(2,1)}, u32[]{:S(2)}, u32[]{:S(2)}) async-start(bf16[16,2,272,128]{3,2,1,0:T(8,128)(2,1)} %shard_map.128), calls=%async_computation.1 | async-start | bytes 4456448 | tf_op jit(solution)/shard_map/all_to_all | solution.py:325
  101.3 4.6 %mul.324 = f32[1,3,256,1024]{3,2,1,0:T(8,128)} reshape(f32[768,8,128]{2,1,0:T(8,128)} %mul.323) | data formatting | bytes 6291456 | tf_op jit(solution)/shard_map/mul | solution.py:43
  108.0 4.6 %mul.331 = f32[1,3,256,1024]{3,2,1,0:T(8,128)} reshape(f32[768,8,128]{2,1,0:T(8,128)} %mul.330) | data formatting | bytes 6291456 | tf_op jit(solution)/shard_map/mul | solution.py:43
  112.8 3.9 %select_convert_fusion = (bf16[1,3,256,1024]{3,2,1,0:T(8,128)(2,1)S(1)}, f32[1,3,256,1024]{3,2,1,0:T(8,128)S(1)}) fusion(pred[1,3,256,1024]{3,2,1,0:T(8,128)(4,1)S(1)} %broadcast_in_dim.41, f32[1024]{0:T(1024)S(1)} %get-tuple-element.45, f32[1,3,256,1024]{3,2,1,0:T(8,128)} %mul.324, f32[1,3,256,1024]{3,2,1,0:T(8,128)} %mul.331, ...), kind=kLoop, calls=%fused_computation.4 | loop fusion | flops 12582912 | bytes 11812864 | tf_op jit(solution)/shard_map/convert_element_type | solution.py:266
  120.3 14.2 %shard_map.129.drive_ref = f32[4096,1024]{1,0:T(8,128)} custom-call(bf16[1,272,2176]{2,1,0:T(8,128)(2,1)} %bitcast.71, bf16[1,3,256,1024]{3,2,1,0:T(8,128)(2,1)} %copy-done.8), custom_call_target="tpu_custom_call" | custom-call | flops 6442450944 | bytes 16777216 | tf_op jit(solution)/shard_map/pallas_call | solution.py:215
  134.5 14.0 %all-to-all-done.1 = bf16[16,2,272,128]{3,2,1,0:T(8,128)(2,1)} async-done(((bf16[16,2,272,128]{3,2,1,0:T(8,128)(2,1)}), bf16[16,2,272,128]{3,2,1,0:T(8,128)(2,1)}, u32[]{:S(2)}, u32[]{:S(2)}) %all-to-all-start.1) | async-done | bytes 2228256 | tf_op jit(solution)/shard_map/all_to_all | solution.py:325
  150.6 2.7 %collective-permute-start.6 = (bf16[2,272,8]{2,1,0:T(8,128)(2,1)S(1)}, bf16[2,272,8]{2,1,0:T(8,128)(2,1)S(1)}, u32[]{:S(2)}, u32[]{:S(2)}) collective-permute-start(bf16[2,272,8]{2,1,0:T(8,128)(2,1)S(1)} %get-tuple-element.32), channel_id=1, source_target_pairs={{16,0},{17,1},{18,2},{19,3},{20,4},{21,5},{22,6},{23,7},{24,8},{25... | collective-permute-start | bytes 26120 | tf_op jit(solution)/shard_map/ppermute | solution.py:340
  155.5 4.1 %collective-permute-done.5 = bf16[2,272,8]{2,1,0:T(8,128)(2,1)S(1)} collective-permute-done((bf16[2,272,8]{2,1,0:T(8,128)(2,1)S(1)}, bf16[2,272,8]{2,1,0:T(8,128)(2,1)S(1)}, u32[]{:S(2)}, u32[]{:S(2)}) %collective-permute-start.5) | collective-permute-done | bytes 8736 | tf_op jit(solution)/shard_map/ppermute | solution.py:339
  159.6 4.0 %concatenate.15 = bf16[2,272,2176]{2,1,0:T(8,128)(2,1)} concatenate(bf16[2,272,8]{2,1,0:T(8,128)(2,1)S(1)} %collective-permute-done.5, bf16[2,272,2048]{2,1,0:T(8,128)(2,1)S(1)} %copy_bitcast_fusion.1, bf16[2,272,8]{2,1,0:T(8,128)(2,1)S(1)} %collective-permute-done.6, bf16[2,272,112]{2,1,0:T(8,128)(2,1)S(1)} %broadcast_in_dim.42), dimensions={2} | concatenate | bytes 4734976 | tf_op jit(solution)/shard_map/concatenate | solution.py:341
  169.2 23.2 %shard_map.130 = f32[256,2048]{1,0:T(8,128)} custom-call(bf16[2,272,2176]{2,1,0:T(8,128)(2,1)} %pad_maximum_fusion.1.term_ref, bf16[2,3,256,1024]{3,2,1,0:T(8,128)(2,1)} %pad_maximum_fusion.band_ref, f32[4096,1024]{1,0:T(8,128)} %shard_map.129.drive_ref), custom_call_target="tpu_custom_call" | custom-call | flops 12884901888 | bytes 16777216 | tf_op jit(solution)/shard_map/pallas_call | solution.py:215
  192.4 2.9 %copy.20 = f32[2048,256]{1,0:T(8,128)} copy(f32[2048,256]{0,1:T(8,128)} %bitcast.70) | data formatting | bytes 4194304 | tf_op jit(solution)/shard_map/transpose | solution.py:357
  (78 shorter events, 28.2 us)
Async XLA Ops:
  0.0 34.7 %copy-start = (f32[16,128,128]{2,1,0:T(8,128)S(1)}, f32[16,128,128]{2,1,0:T(8,128)}, u32[]{:S(2)}) copy-start(f32[16,128,128]{2,1,0:T(8,128)} %param.14) | copy-start | bytes 3145732
  0.8 26.8 %collective-permute-start.4 = (s32[2,4]{1,0:T(2,128)S(1)}, s32[2,4]{1,0:T(2,128)S(1)}, u32[]{:S(2)}, u32[]{:S(2)}) collective-permute-start(s32[2,4]{1,0:T(2,128)S(1)} %pad_add_fusion.2), channel_id=1, source_target_pairs={{0,1},{1,0},{2,3},{3,2},{4,5},{5,4},{6,7},{7,6},{8,9},{9,8},{10,11... | collective-permute-start | bytes 104 | tf_op jit(solution)/shard_map/ppermute | solution.py:287
  2.8 18.2 %collective-permute-start = (s32[1,4]{0,1:T(4,128)S(1)}, s32[1,4]{0,1:T(4,128)S(1)}, u32[]{:S(2)}, u32[]{:S(2)}) collective-permute-start(s32[1,4]{0,1:T(4,128)S(1)} %get-tuple-element.36), channel_id=1, source_target_pairs={{0,16},{1,17},{2,18},{3,19},{4,20},{5,21},{6,22},{7,23},{8,24},{9,... | collective-permute-start | bytes 56 | tf_op jit(solution)/shard_map/ppermute | solution.py:239
  4.1 16.9 %collective-permute-start.1 = (s32[1,4]{0,1:T(4,128)S(1)}, s32[1,4]{0,1:T(4,128)S(1)}, u32[]{:S(2)}, u32[]{:S(2)}) collective-permute-start(s32[1,4]{0,1:T(4,128)S(1)} %get-tuple-element.37), channel_id=1, source_target_pairs={{16,0},{17,1},{18,2},{19,3},{20,4},{21,5},{22,6},{23,7},{24,8},{25... | collective-permute-start | bytes 56 | tf_op jit(solution)/shard_map/ppermute | solution.py:240
  9.6 2.8 %copy-start.2 = (bf16[256,256]{1,0:T(8,128)(2,1)S(1)}, bf16[256,256]{1,0:T(8,128)(2,1)}, u32[]{:S(2)}) copy-start(bf16[256,256]{1,0:T(8,128)(2,1)} %constant.92.clone.small_ref) | copy-start | bytes 393220
  9.6 2.8 %copy-start.3 = (bf16[256,256]{1,0:T(8,128)(2,1)S(1)}, bf16[256,256]{1,0:T(8,128)(2,1)}, u32[]{:S(2)}) copy-start(bf16[256,256]{1,0:T(8,128)(2,1)} %constant.91.clone.big_ref) | copy-start | bytes 393220
  9.6 2.8 %copy-start.4 = (f32[32,128]{1,0:T(8,128)S(1)}, f32[32,128]{1,0:T(8,128)}, u32[]{:S(2)}) copy-start(f32[32,128]{1,0:T(8,128)} %constant.90.clone.sin_ref) | copy-start | bytes 49156
  9.6 2.8 %copy-start.5 = (f32[32,128]{1,0:T(8,128)S(1)}, f32[32,128]{1,0:T(8,128)}, u32[]{:S(2)}) copy-start(f32[32,128]{1,0:T(8,128)} %constant.89.clone.cos_ref) | copy-start | bytes 49156
  12.4 8.6 %copy-start.9 = (s32[16,4]{0,1:T(4,128)S(1)}, s32[16,4]{0,1:T(4,128)}, u32[]{:S(2)}) copy-start(s32[16,4]{0,1:T(4,128)} %param.15) | copy-start | bytes 772
  12.4 15.2 %copy-start.10 = (s32[4]{0:T(128)S(1)}, s32[4]{0:T(128)}, u32[]{:S(2)}) copy-start(s32[4]{0:T(128)} %param.17) | copy-start | bytes 52
  12.4 15.2 %copy-start.11 = (s32[4]{0:T(128)S(1)}, s32[4]{0:T(128)}, u32[]{:S(2)}) copy-start(s32[4]{0:T(128)} %param.16) | copy-start | bytes 52
  21.1 6.6 %collective-permute-start.2 = (s32[18,1]{0,1:T(1,128)S(1)}, s32[18,1]{0,1:T(1,128)S(1)}, u32[]{:S(2)}, u32[]{:S(2)}) collective-permute-start(s32[18,1]{0,1:T(1,128)S(1)} %get-tuple-element.34), channel_id=1, source_target_pairs={{0,2},{2,4},{4,6},{6,8},{8,10},{10,12},{12,14},{1,3},{3,5},{5,7},{... | collective-permute-start | bytes 224 | tf_op jit(solution)/shard_map/ppermute | solution.py:239
  25.7 4.9 %collective-permute-start.3 = (s32[18,1]{0,1:T(1,128)S(1)}, s32[18,1]{0,1:T(1,128)S(1)}, u32[]{:S(2)}, u32[]{:S(2)}) collective-permute-start(s32[18,1]{0,1:T(1,128)S(1)} %get-tuple-element.35), channel_id=1, source_target_pairs={{2,0},{4,2},{6,4},{8,6},{10,8},{12,10},{14,12},{3,1},{5,3},{7,5},{... | collective-permute-start | bytes 224 | tf_op jit(solution)/shard_map/ppermute | solution.py:240
  30.6 49.6 %all-to-all-start = ((bf16[32,2,128,128]{3,2,1,0:T(8,128)(2,1)}), bf16[32,2,128,128]{3,2,1,0:T(8,128)(2,1)S(1)}, u32[]{:S(2)}, u32[]{:S(2)}) async-start(bf16[32,2,128,128]{3,2,1,0:T(8,128)(2,1)} %shard_map.127), calls=%async_computation | async-start | bytes 4194304 | tf_op jit(solution)/shard_map/all_to_all | solution.py:298
  89.2 59.3 %all-to-all-start.1 = ((bf16[16,2,272,128]{3,2,1,0:T(8,128)(2,1)}), bf16[16,2,272,128]{3,2,1,0:T(8,128)(2,1)}, u32[]{:S(2)}, u32[]{:S(2)}) async-start(bf16[16,2,272,128]{3,2,1,0:T(8,128)(2,1)} %shard_map.128), calls=%async_computation.1 | async-start | bytes 4456448 | tf_op jit(solution)/shard_map/all_to_all | solution.py:325
  118.1 2.2 %copy-start.8 = (bf16[1,3,256,1024]{3,2,1,0:T(8,128)(2,1)}, bf16[1,3,256,1024]{3,2,1,0:T(8,128)(2,1)S(1)}, u32[]{:S(2)}) copy-start(bf16[1,3,256,1024]{3,2,1,0:T(8,128)(2,1)S(1)} %select_convert_fusion.1.band_ref) | copy-start | bytes 4718596
  150.6 4.9 %collective-permute-start.6 = (bf16[2,272,8]{2,1,0:T(8,128)(2,1)S(1)}, bf16[2,272,8]{2,1,0:T(8,128)(2,1)S(1)}, u32[]{:S(2)}, u32[]{:S(2)}) collective-permute-start(bf16[2,272,8]{2,1,0:T(8,128)(2,1)S(1)} %get-tuple-element.32), channel_id=1, source_target_pairs={{16,0},{17,1},{18,2},{19,3},{20,4},{21,5},{22,6},{23,7},{24,8},{25... | collective-permute-start | bytes 26120 | tf_op jit(solution)/shard_map/ppermute | solution.py:340
  153.3 6.3 %collective-permute-start.5 = (bf16[2,272,8]{2,1,0:T(8,128)(2,1)S(1)}, bf16[2,272,8]{2,1,0:T(8,128)(2,1)S(1)}, u32[]{:S(2)}, u32[]{:S(2)}) collective-permute-start(bf16[2,272,8]{2,1,0:T(8,128)(2,1)S(1)} %get-tuple-element.33), channel_id=1, source_target_pairs={{0,16},{1,17},{2,18},{3,19},{4,20},{5,21},{6,22},{7,23},{8,24},{9,... | collective-permute-start | bytes 26120 | tf_op jit(solution)/shard_map/ppermute | solution.py:339
  163.6 2.4 %copy-start.6 = (f32[272,2176]{1,0:T(8,128)S(1)}, f32[272,2176]{1,0:T(8,128)}, u32[]{:S(2)}) copy-start(f32[272,2176]{1,0:T(8,128)} %get-tuple-element.22) | copy-start | bytes 7102468
  163.6 3.1 %copy-start.7 = (f32[272,2176]{1,0:T(8,128)S(1)}, f32[272,2176]{1,0:T(8,128)}, u32[]{:S(2)}) copy-start(f32[272,2176]{1,0:T(8,128)} %get-tuple-element.21) | copy-start | bytes 7102468
  169.2 26.1 %copy-start.1 = (f32[16,128,128]{2,1,0:T(8,128)S(1)}, f32[16,128,128]{2,1,0:T(8,128)}, u32[]{:S(2)}) copy-start(f32[16,128,128]{2,1,0:T(8,128)} %param.14) | copy-start | bytes 3145732
